TPU v7x, 32 devices: a whole 2x2x4 slice. The times are simulated.
32 devices in a mesh: seq: 4 (over y, x), exp: 8 (over z, core).
Axes of the slice: x: 2, y: 2, z: 4, core: 2. Of those that a mesh axis runs over, the one named last changes fastest.
Arguments:
- inputs: bfloat16 [4096, 4096], P(('seq', 'exp')), may hold values from -6 to 6
- queries: bfloat16 [4096, 4096], P(('seq', 'exp')), may hold values from -40 to 40
- keys: bfloat16 [4096, 4096], P(('seq', 'exp')), may hold values from -4 to 4
- values: bfloat16 [4096, 4096], P(('seq', 'exp')), may hold values from -6 to 6
- norm_gain: float32 [4096], replicated, may hold values from 0.25 to 1.75
- expert_ids: int32 [4096, 2], P(('seq', 'exp')), may hold values from 0 to 7, all different within a row; in each aligned block of 128 rows (0 to 127, 128 to 255, ...) at most 32 rows name the same one
- gate_weights: float32 [4096, 2], P(('seq', 'exp')), may hold values from 0.2 to 1
- pairs: int32 [16, 2], replicated, may hold values from 0 to 7, as said below
- w_gate: bfloat16 [8, 4096, 4096], P('exp', None, 'seq'), may hold values from -0.09375 to 0.09375
- w_up: bfloat16 [8, 4096, 4096], P('exp', None, 'seq'), may hold values from -0.09375 to 0.09375
- w_down: bfloat16 [8, 4096, 4096], P('exp', 'seq'), may hold values from -0.09375 to 0.09375
Outputs:
- output: bfloat16 [4096, 4096], P(('seq', 'exp'))
Inputs may be any that keep to these rules, and one draw needn't show every extreme that they name: `pairs`: each row is (query block, key block) with the key block from the query block - 2 to the query block; rows are distinct; every block is paired with itself; some pair has distance 2. `expert_ids`: the 2 ids of a token differ; within the 128 rows of one device every expert is named exactly 32 times.
All inputs are finite; a program needn't handle non-finite values.
Results may differ from a plain program's by a relative error of at most 0.007.
Values may be sent and summed in bfloat16 or wider, within the bound.
A program may use at most 128 MiB of HBM per device.

v0:
```python
import math

import jax
import jax.numpy as jnp
from jax import lax
from jax.sharding import PartitionSpec as P

HSZ = 128
TOP = 2
BLK = 512
DIST = 2


very_negative = -1e30
norm_epsilon = 1e-05


def from_behind(value, axis, steps):
    count = lax.axis_size(axis)
    leading, last = (max(0, -steps), min(count, count - steps))
    return lax.ppermute(value, axis, [(source, source + steps) for source in range(leading, last)])


def expert_part(flat_rows, gate_slice, up_slice, down_slice):
    gate_value = jnp.dot(flat_rows, gate_slice, preferred_element_type=jnp.float32)
    up_value = jnp.dot(flat_rows, up_slice, preferred_element_type=jnp.float32)
    hidden = (jax.nn.silu(gate_value) * up_value).astype(jnp.bfloat16)
    return jnp.dot(hidden, down_slice, preferred_element_type=jnp.float32)


def block_present(pairs, query_block, distance):
    matches = (pairs[:, 0] == query_block) & (pairs[:, 1] == query_block - distance)
    return jnp.any(matches)


def per_device(
    inputs, queries, keys, values, norm_gain, expert_ids, gate_weights, pairs, w_gate, w_up, w_down
):
    rows_dev, model_width = inputs.shape
    exp_count = lax.axis_size("exp")
    score_scale = 1.0 / math.sqrt(HSZ)
    query_run, key_run, value_run = (
        lax.all_to_all(queries, "exp", split_axis=1, concat_axis=0, tiled=True),
        lax.all_to_all(keys, "exp", split_axis=1, concat_axis=0, tiled=True),
        lax.all_to_all(values, "exp", split_axis=1, concat_axis=0, tiled=True),
    )
    run_rows, group_width = query_run.shape
    heads_dev = group_width // HSZ
    tail_rows = DIST * BLK
    keys_prev, values_prev = from_behind(
        (key_run[run_rows - tail_rows :], value_run[run_rows - tail_rows :]), "seq", 1
    )
    keys_ext = jnp.concatenate([keys_prev, key_run], 0).reshape(-1, heads_dev, HSZ)
    values_ext = jnp.concatenate([values_prev, value_run], 0).reshape(-1, heads_dev, HSZ)
    blocks_dev = run_rows // BLK
    first_block = lax.axis_index("seq") * blocks_dev
    attended_blocks = []
    for local_block in range(blocks_dev):
        query_block = first_block + local_block
        query_rows = query_run[local_block * BLK : (local_block + 1) * BLK].reshape(
            BLK, heads_dev, HSZ
        )
        present = [
            block_present(pairs, query_block, DIST - key_slot) for key_slot in range(DIST + 1)
        ]
        window_start = tail_rows + (local_block - DIST) * BLK
        window_end = window_start + (DIST + 1) * BLK
        scores = (
            jnp.einsum(
                "qhd,khd->hqk",
                query_rows,
                keys_ext[window_start:window_end],
                preferred_element_type=jnp.float32,
            )
            * score_scale
        )
        key_mask = jnp.repeat(jnp.stack(present), BLK)
        scores = jnp.where(key_mask[None, None, :], scores, very_negative)
        row_top = jnp.max(scores, axis=2, keepdims=True)
        exp_scores = jnp.exp(scores - row_top)
        denominator = jnp.sum(exp_scores, axis=2)
        weights = exp_scores.astype(jnp.bfloat16)
        summed = jnp.einsum(
            "hqk,khd->qhd",
            weights,
            values_ext[window_start:window_end],
            preferred_element_type=jnp.float32,
        )
        attended_block = (summed / jnp.transpose(denominator)[:, :, None]).astype(jnp.bfloat16)
        attended_blocks.append(attended_block.reshape(BLK, group_width))
    attended_run = jnp.concatenate(attended_blocks, 0)
    attended = lax.all_to_all(attended_run, "exp", split_axis=0, concat_axis=1, tiled=True)
    mixed_sum = inputs.astype(jnp.float32) + attended.astype(jnp.float32)
    mean_square = jnp.mean(mixed_sum * mixed_sum, axis=1, keepdims=True)
    normed = (mixed_sum * lax.rsqrt(mean_square + norm_epsilon) * norm_gain[None, :]).astype(
        jnp.bfloat16
    )
    capacity = rows_dev * TOP // exp_count
    flat_ids = expert_ids.reshape(-1)
    assignments = flat_ids.shape[0]
    id_table = (flat_ids[:, None] == jnp.arange(exp_count, dtype=jnp.int32)[None, :]).astype(
        jnp.int32
    )
    ahead_count = jnp.cumsum(id_table, axis=0) - id_table
    position = jnp.sum(ahead_count * id_table, axis=1)
    target = flat_ids * capacity + position
    source = (
        jnp.zeros((exp_count * capacity,), jnp.int32)
        .at[target]
        .set(jnp.arange(assignments, dtype=jnp.int32))
    )
    outgoing = normed[source // TOP].reshape(exp_count, capacity, model_width)
    gate_slice = w_gate[0]
    up_slice = w_up[0]
    down_slice = w_down[0]
    piece_rows = lax.all_gather(
        lax.all_to_all(outgoing, "exp", split_axis=0, concat_axis=0, tiled=True),
        "seq",
        axis=0,
        tiled=True,
    )
    flat_rows = piece_rows.reshape(-1, model_width)
    slice_parts = expert_part(flat_rows, gate_slice, up_slice, down_slice).reshape(piece_rows.shape)
    slice_total = lax.psum_scatter(
        slice_parts.astype(jnp.bfloat16), "seq", scatter_dimension=0, tiled=True
    ).astype(jnp.float32)
    expert_out = lax.all_to_all(
        slice_total.astype(jnp.bfloat16), "exp", split_axis=0, concat_axis=0, tiled=True
    ).astype(slice_total.dtype)
    gathered = expert_out.reshape(exp_count * capacity, model_width)[target].reshape(
        rows_dev, TOP, model_width
    )
    output = mixed_sum + jnp.sum(gate_weights[:, :, None] * gathered, axis=1)
    return output.astype(jnp.bfloat16)


def solution(mesh):
    in_specs = (
        P(("seq", "exp"), None),
        P(("seq", "exp"), None),
        P(("seq", "exp"), None),
        P(("seq", "exp"), None),
        P(),
        P(("seq", "exp"), None),
        P(("seq", "exp"), None),
        P(),
        P("exp", None, "seq"),
        P("exp", None, "seq"),
        P("exp", "seq", None),
    )
    out_specs = P(("seq", "exp"), None)
    return jax.shard_map(
        per_device, mesh=mesh, in_specs=in_specs, out_specs=out_specs, check_vma=False
    )
```

profile of v0, /device:TPU:0, one launch (start us, length us, event | category | flops | bytes accessed | tf_op | source)
XLA Modules:
  0.0 532.3 jit_solution(13733365971950306756)
XLA Ops:
  6.5 1.7 copy.68
  8.2 1.3 copy.69
  9.6 6.4 %all-to-all-start = ((bf16[128,8,512]{2,0,1:T(8,128)(2,1)}), bf16[128,8,512]{2,0,1:T(8,128)(2,1)S(1)}, u32[]{:S(2)}, u32[]{:S(2)}) async-start(bf16[128,8,512]{2,0,1:T(8,128)(2,1)} %copy.69), calls=%async_computation | async-start | bytes 2097152 | tf_op jit(solution)/shard_map/all_to_all | solution.py:45
  15.9 1.3 copy.72
  17.3 25.2 %all-to-all-done = bf16[128,8,512]{2,0,1:T(8,128)(2,1)S(1)} async-done(((bf16[128,8,512]{2,0,1:T(8,128)(2,1)}), bf16[128,8,512]{2,0,1:T(8,128)(2,1)S(1)}, u32[]{:S(2)}, u32[]{:S(2)}) %all-to-all-start) | async-done | bytes 1048608 | tf_op jit(solution)/shard_map/all_to_all | solution.py:45
  42.5 3.7 all-to-all-start.1
  46.2 2.3 copy.104
  48.5 24.2 %all-to-all-done.1 = bf16[128,8,512]{0,2,1:T(8,128)(2,1)S(1)} async-done(((bf16[128,8,512]{0,2,1:T(8,128)(2,1)}), bf16[128,8,512]{0,2,1:T(8,128)(2,1)S(1)}, u32[]{:S(2)}, u32[]{:S(2)}) %all-to-all-start.1) | async-done | bytes 1048608 | tf_op jit(solution)/shard_map/all_to_all | solution.py:44
  72.7 3.6 all-to-all-start.2
  76.2 1.5 copy.73
  77.7 4.4 collective-permute-start.1
  82.1 0.8 and_reduce_fusion.5
  82.9 2.0 pad_add_fusion.1
  84.9 1.9 pad_add_fusion
  86.9 0.1 broadcast_in_dim.41
  87.0 1.3 copy.70
  88.3 3.5 collective-permute-start
  91.8 11.0 %all-to-all-done.2 = bf16[128,8,512]{2,0,1:T(8,128)(2,1)S(1)} async-done(((bf16[128,8,512]{2,0,1:T(8,128)(2,1)}), bf16[128,8,512]{2,0,1:T(8,128)(2,1)S(1)}, u32[]{:S(2)}, u32[]{:S(2)}) %all-to-all-start.2) | async-done | bytes 1048608 | tf_op jit(solution)/shard_map/all_to_all | solution.py:43
  102.8 0.9 reshape.135
  103.7 0.9 reshape.133
  104.7 2.8 fusion.23
  107.4 1.7 copy.79
  109.1 7.3 %bitcast_reduce_fusion = (f32[4,512]{1,0:T(4,128)S(1)}, f32[4,1536,512]{2,1,0:T(8,128)}) fusion(pred[1536]{0:T(1024)(128)(4,1)S(1)} %broadcast_in_dim.46, bf16[1536,4,128]{0,2,1:T(8,128)(2,1)S(1)} %bitcast.108, bf16[512,4,128]{2,1,0:T(4,128)(2,1)} %reshape.135), kind=kOutput, calls=%fused_computation.4 | convolution fusion | flops 814741504 | bytes 14689792 | tf_op jit(solution)/shard_map/qhd,khd->hqk/dot_general | solution.py:69
  116.4 0.7 copy.74
  117.1 7.0 %fusion.4 = f32[4,512]{1,0:T(4,128)S(1)} fusion(f32[4,1536,512]{2,1,0:T(8,128)} %get-tuple-element.18, f32[4,512]{1,0:T(4,128)S(1)} %get-tuple-element.17, pred[1536]{0:T(1024)(128)(4,1)S(1)} %broadcast_in_dim.46), kind=kLoop, calls=%fused_computation.13 | loop fusion | flops 12580864 | bytes 12600832 | tf_op jit(solution)/shard_map/reduce_sum | solution.py:81
  124.1 2.6 collective-permute-done
  126.7 2.2 fusion.24
  128.9 3.2 divide_convert_fusion
  132.1 3.0 bitcast_reduce_fusion.1
  135.1 3.6 fusion.2
  138.7 3.2 divide_convert_fusion.1
  141.9 0.1 pad_maximum_fusion.2
  142.1 1.3 copy.83
  143.4 4.7 all-to-all-start.3
  148.2 0.1 copy.87
  148.3 0.1 eq.89
  148.5 0.1 eq.85
  148.6 0.1 copy.86
  148.7 0.1 mul.75
  148.9 0.6 reduce-window.6
  149.5 0.2 slice_reduce_fusion
  149.7 0.1 fusion.40
  149.8 1.4 scatter_custom_fusion
  151.3 23.4 %all-to-all-done.3 = bf16[8,128,512]{2,1,0:T(8,128)(2,1)S(1)} async-done(((bf16[8,128,512]{2,1,0:T(8,128)(2,1)}), bf16[8,128,512]{2,1,0:T(8,128)(2,1)S(1)}, u32[]{:S(2)}, u32[]{:S(2)}) %all-to-all-start.3) | async-done | bytes 1048608 | tf_op jit(solution)/shard_map/all_to_all | solution.py:92
  174.7 0.3 convert_bitcast_fusion
  175.0 0.2 copy.94
  175.2 0.4 multiply_reduce_fusion.1
  175.6 0.6 copy-done.2
  176.2 0.4 multiply_convert_fusion.1
  176.6 3.2 gather_fusion
  179.8 53.4 %all_to_all.77 = bf16[8,32,4096]{2,1,0:T(8,128)(2,1)} all-to-all(bf16[8,32,4096]{2,1,0:T(8,128)(2,1)} %bitcast.109), channel_id=1, replica_groups=mesh['seq'=4,'exp'=8] {'exp'}, dimensions={0} | all-to-all | bytes 4194304 | tf_op jit(solution)/shard_map/all_to_all | solution.py:117
  233.3 87.5 %all-gather.2.cloned.1.call-done = bf16[32,32,4096]{2,1,0:T(8,128)(2,1)} async-done(((bf16[8,32,4096]{2,1,0:T(8,128)(2,1)}), bf16[32,32,4096]{2,1,0:T(8,128)(2,1)}) %all-gather.2.cloned.1.call-update) | async-done | bytes 8388624 | tf_op jit(solution)/shard_map/all_gather | solution.py:116
  320.8 12.9 %fusion.8 = f32[1024,1024]{1,0:T(8,128)S(1)} fusion(bf16[1024,4096]{1,0:T(8,128)(2,1)} %bitcast.128, bf16[1,4096,1024]{2,1,0:T(8,128)(2,1)} %param.20), kind=kOutput, calls=%fused_computation.17 | convolution fusion | flops 8589934592 | bytes 20971520 | tf_op jit(solution)/shard_map/dot_general | solution.py:26
  333.7 12.0 %multiply_convert_fusion = bf16[1024,1024]{1,0:T(8,128)(2,1)S(1)} fusion(f32[1024,1024]{1,0:T(8,128)S(1)} %fusion.8, bf16[1024,4096]{1,0:T(8,128)(2,1)S(1)} %bitcast.129, bf16[1,4096,1024]{2,1,0:T(8,128)(2,1)} %param.19), kind=kOutput, calls=%fused_computation.27 | convolution fusion | flops 8596226048 | bytes 23068672 | tf_op jit(solution)/shard_map/dot_general | solution.py:25
  345.7 11.0 %fusion.12 = bf16[32,32,4096]{2,1,0:T(8,128)(2,1)} fusion(bf16[32,32,1024]{2,1,0:T(8,128)(2,1)S(1)} %bitcast.130, bf16[1,1024,4096]{2,1,0:T(8,128)(2,1)S(1)} %bitcast.127), kind=kOutput, calls=%fused_computation.21 | convolution fusion | flops 8594128896 | bytes 18874368 | tf_op jit(solution)/shard_map/dot_general | solution.py:28
  356.7 86.5 %reduce-scatter.2.cloned.1.call-done = bf16[8,32,4096]{2,1,0:T(8,128)(2,1)} async-done(((bf16[32,32,4096]{2,1,0:T(8,128)(2,1)}), bf16[8,32,4096]{2,1,0:T(8,128)(2,1)}) %reduce-scatter.2.cloned.1.call-update) | async-done | bytes 2097168 | tf_op jit(solution)/shard_map/reduce_scatter | solution.py:124
  443.2 4.9 all-to-all-start.5
  448.1 0.1 copy.85
  448.2 48.9 %all-to-all-done.5 = bf16[8,32,4096]{2,1,0:T(8,128)(2,1)} async-done(((bf16[8,32,4096]{2,1,0:T(8,128)(2,1)}), bf16[8,32,4096]{2,1,0:T(8,128)(2,1)}, u32[]{:S(2)}, u32[]{:S(2)}) %all-to-all-start.5) | async-done | bytes 2097184 | tf_op jit(solution)/shard_map/all_to_all | solution.py:127
  497.2 4.0 bitcast_convert_fusion
  501.2 7.8 %gather_fusion.1 = f32[256,4096]{1,0:T(8,128)} fusion(f32[256,4096]{1,0:T(8,128)} %bitcast_convert_fusion, s32[1024]{0:T(1024)S(1)} %pad_clamp_fusion), kind=kCustom, calls=%fused_computation.1 | custom fusion | bytes 8389632 | tf_op jit(solution)/shard_map/gather | solution.py:130
  509.0 5.8 %reshape.142 = f32[128,2,4096]{2,1,0:T(2,128)} reshape(f32[256,4096]{1,0:T(8,128)} %gather_fusion.1) | data formatting | bytes 8388608 | tf_op jit(solution)/shard_map/reshape | solution.py:130
  514.8 8.8 %multiply_reduce_fusion = f32[128,4096]{1,0:T(8,128)S(1)} fusion(f32[128,2,4096]{2,1,0:T(2,128)} %reshape.142, f32[128,2]{1,0:T(8,128)S(1)} %copy.85), kind=kLoop, calls=%fused_computation.26 | loop fusion | flops 1572864 | bytes 6292480 | tf_op jit(solution)/shard_map/reduce_sum | solution.py:133
  523.7 1.4 add_convert_fusion
  (47 shorter events, 0.5 us)
Async XLA Ops:
  6.5 9.4 %copy-start.6 = (bf16[128,4096]{1,0:T(8,128)(2,1)S(1)}, bf16[128,4096]{1,0:T(8,128)(2,1)}, u32[]{:S(2)}) copy-start(bf16[128,4096]{1,0:T(8,128)(2,1)} %param.13) | copy-start | bytes 3145732
  9.6 32.9 %all-to-all-start = ((bf16[128,8,512]{2,0,1:T(8,128)(2,1)}), bf16[128,8,512]{2,0,1:T(8,128)(2,1)S(1)}, u32[]{:S(2)}, u32[]{:S(2)}) async-start(bf16[128,8,512]{2,0,1:T(8,128)(2,1)} %copy.69), calls=%async_computation | async-start | bytes 2097152 | tf_op jit(solution)/shard_map/all_to_all | solution.py:45
  42.5 39.6 %copy-start.10 = (s32[16,2]{0,1:T(2,128)S(1)}, s32[16,2]{0,1:T(2,128)}, u32[]{:S(2)}) copy-start(s32[16,2]{0,1:T(2,128)} %param.18) | copy-start | bytes 388
  42.5 30.2 %all-to-all-start.1 = ((bf16[128,8,512]{0,2,1:T(8,128)(2,1)}), bf16[128,8,512]{0,2,1:T(8,128)(2,1)S(1)}, u32[]{:S(2)}, u32[]{:S(2)}) async-start(bf16[128,8,512]{0,2,1:T(8,128)(2,1)} %bitcast.8), calls=%async_computation.1 | async-start | bytes 2097152 | tf_op jit(solution)/shard_map/all_to_all | solution.py:44
  72.7 3.6 copy-start.4
  72.7 30.1 %all-to-all-start.2 = ((bf16[128,8,512]{2,0,1:T(8,128)(2,1)}), bf16[128,8,512]{2,0,1:T(8,128)(2,1)S(1)}, u32[]{:S(2)}, u32[]{:S(2)}) async-start(bf16[128,8,512]{2,0,1:T(8,128)(2,1)} %bitcast.103), calls=%async_computation.2 | async-start | bytes 2097152 | tf_op jit(solution)/shard_map/all_to_all | solution.py:43
  77.7 26.9 %collective-permute-start.1 = (bf16[1024,512]{1,0:T(8,128)(2,1)S(1)}, bf16[1024,512]{1,0:T(8,128)(2,1)}, u32[]{:S(2)}, u32[]{:S(2)}) collective-permute-start(bf16[1024,512]{1,0:T(8,128)(2,1)S(1)} %bitcast.110), channel_id=1, source_target_pairs={{0,8},{8,16},{16,24},{1,9},{9,17},{17,25},{2,10},{10,18},{18,26},{... | collective-permute-start | bytes 3145736 | tf_op jit(solution)/shard_map/ppermute | solution.py:21
  88.3 38.4 %collective-permute-start = (bf16[1024,512]{0,1:T(8,128)(2,1)}, bf16[1024,512]{0,1:T(8,128)(2,1)}, u32[]{:S(2)}, u32[]{:S(2)}) collective-permute-start(bf16[1024,512]{0,1:T(8,128)(2,1)} %copy.70), channel_id=1, source_target_pairs={{0,8},{8,16},{16,24},{1,9},{9,17},{17,25},{2,10},{10,18},{18,26},{... | collective-permute-start | bytes 3145736 | tf_op jit(solution)/shard_map/ppermute | solution.py:21
  117.1 11.7 %copy-start = (f32[4,1536,512]{2,1,0:T(8,128)S(1)}, f32[4,1536,512]{2,1,0:T(8,128)}, u32[]{:S(2)}) copy-start(f32[4,1536,512]{2,1,0:T(8,128)} %get-tuple-element.18) | copy-start | bytes 37748740
  128.9 3.2 copy-start.5
  141.9 6.3 %copy-start.8 = (s32[128,2]{0,1:T(2,128)S(1)}, s32[128,2]{0,1:T(2,128)}, u32[]{:S(2)}) copy-start(s32[128,2]{0,1:T(2,128)} %param.16) | copy-start | bytes 3076
  143.4 31.3 %all-to-all-start.3 = ((bf16[8,128,512]{2,1,0:T(8,128)(2,1)}), bf16[8,128,512]{2,1,0:T(8,128)(2,1)S(1)}, u32[]{:S(2)}, u32[]{:S(2)}) async-start(bf16[8,128,512]{2,1,0:T(8,128)(2,1)} %bitcast.26), calls=%async_computation.3 | async-start | bytes 2097152 | tf_op jit(solution)/shard_map/all_to_all | solution.py:92
  148.1 27.1 %copy-start.1 = (bf16[128,4096]{1,0:T(8,128)(2,1)S(1)}, bf16[128,4096]{1,0:T(8,128)(2,1)}, u32[]{:S(2)}) copy-start(bf16[128,4096]{1,0:T(8,128)(2,1)} %param.11) | copy-start | bytes 3145732
  148.2 172.6 %all-gather.2.cloned.1.call-start = ((), (), s32[]{:S(2)}) async-start(), calls=%async_computation.7 | async-start | bytes 10485760 | tf_op jit(solution)/shard_map/all_gather | solution.py:116
  175.0 1.2 copy-start.2
  175.0 1.2 copy-start.7
  233.2 209.9 %reduce-scatter.2.cloned.1.call-start = ((), (), s32[]{:S(2)}) async-start(), calls=%async_computation.8 | async-start | bytes 10485760 | tf_op jit(solution)/shard_map/reduce_scatter | solution.py:124
  320.8 12.9 %copy-start.11 = (bf16[32,32,4096]{2,1,0:T(8,128)(2,1)S(1)}, bf16[32,32,4096]{2,1,0:T(8,128)(2,1)}, u32[]{:S(2)}) copy-start(bf16[32,32,4096]{2,1,0:T(8,128)(2,1)} %all-gather.2.cloned.1.call-done) | copy-start | bytes 25165828
  320.8 24.9 %slice-start = ((s8[8388608]{0:T(1024)(128)(4,1)}), s8[4194304]{0:T(1024)(128)(4,1)S(1)}, s32[]{:S(2)}) async-start(s8[8388608]{0:T(1024)(128)(4,1)} %bitcast.126), calls=%async_computation.9 | async-start | bytes 8388608
  333.7 12.0 %slice-start.1 = ((s8[8388608]{0:T(1024)(128)(4,1)}), s8[4194304]{0:T(1024)(128)(4,1)S(1)}, s32[]{:S(2)}) async-start(s8[8388608]{0:T(1024)(128)(4,1)} %bitcast.126), calls=%async_computation.10 | async-start | bytes 8388608
  356.7 91.4 %copy-start.9 = (f32[128,2]{0,1:T(2,128)S(1)}, f32[128,2]{0,1:T(2,128)}, u32[]{:S(2)}) copy-start(f32[128,2]{0,1:T(2,128)} %param.17) | copy-start | bytes 3076
  443.2 54.0 %all-to-all-start.5 = ((bf16[8,32,4096]{2,1,0:T(8,128)(2,1)}), bf16[8,32,4096]{2,1,0:T(8,128)(2,1)}, u32[]{:S(2)}, u32[]{:S(2)}) async-start(bf16[8,32,4096]{2,1,0:T(8,128)(2,1)} %reduce-scatter.2.cloned.1.call-done), calls=%async_computation.6 | async-start | bytes 4194304 | tf_op jit(solution)/shard_map/all_to_all | solution.py:127
  514.8 8.8 %copy-start.3 = (bf16[128,4096]{1,0:T(8,128)(2,1)S(1)}, bf16[128,4096]{1,0:T(8,128)(2,1)}, u32[]{:S(2)}) copy-start(bf16[128,4096]{1,0:T(8,128)(2,1)} %param.11) | copy-start | bytes 3145732
Sparse Core Ops, SparseCore 0:
  233.3 87.3 all-gather.1
  356.8 86.3 reduce-scatter.1
where the time goes:
time: 543 us; the launch traced here: 532 us
  waiting for transfers between devices  309 us (57%)
  blocking collectives  53.4 us (10%)
  matrix products  52.5 us (10%)
  other arithmetic  36.3 us (7%)
  local copies, waits for them, and re-layouts  35.4 us (7%)
  starting transfers between devices  31.2 us (6%)
  between operations  14.3 us (3%)
    all_gather x1, waiting for transfers between devices, per_device(): lax.all_gather(lax.all_to_all(outgoing, 'exp', split_axis=0, concat_axis=...  87.5 us
    reduce_scatter x1, waiting for transfers between devices, per_device(): lax.psum_scatter(slice_parts.astype(jnp.bfloat16), 'seq', scatter_dimensi...  86.5 us
    all_to_all x1, blocking collectives, per_device(): lax.all_to_all(outgoing, 'exp', split_axis=0, concat_axis=0, tiled=True)  53.4 us
    all_to_all x1, waiting for transfers between devices, per_device(): lax.all_to_all(slice_total.astype(jnp.bfloat16), 'exp', split_axis=0, con...  48.9 us
    all_to_all x1, waiting for transfers between devices, per_device(): lax.all_to_all(values, 'exp', split_axis=1, concat_axis=0, tiled=True)  25.2 us
    all_to_all x1, waiting for transfers between devices, per_device(): lax.all_to_all(keys, 'exp', split_axis=1, concat_axis=0, tiled=True)  24.2 us
    all_to_all x1, waiting for transfers between devices, per_device(): lax.all_to_all(attended_run, 'exp', split_axis=0, concat_axis=1, tiled=True)  23.4 us
    dot_general x1, matrix products, expert_part(): up_value = jnp.dot(flat_rows, up_slice, preferred_element_type=jnp.float32)  12.9 us
  transfers between devices with their start and end apart: 9, of which 9 were waited for; matrix products, arithmetic and copies ran while one was open for 7% of the time, Pallas kernels for 0%

commit v1 on v0

v1 whole, which is shorter than its diff:
```python
import functools
import math

import jax
import jax.numpy as jnp
from jax import lax
from jax.experimental import pallas as pl
from jax.experimental.pallas import tpu as pltpu
from jax.sharding import PartitionSpec as P

HSZ = 128
TOP = 2
BLK = 512
DIST = 2
OUTER = 2
AHEAD = 2

very_negative = -1e30
norm_epsilon = 1e-05

MESH = pl.DeviceIdType.MESH
ANY = pl.BlockSpec(memory_space=pl.ANY)
DMA = pltpu.SemaphoreType.DMA


def remote(source, target, send_sem, recv_sem, device):
    return pltpu.make_async_remote_copy(
        src_ref=source,
        dst_ref=target,
        send_sem=send_sem,
        recv_sem=recv_sem,
        device_id=device,
        device_id_type=MESH,
    )


def enter(peers):
    barrier = pltpu.get_barrier_semaphore()
    for peer in peers:
        pl.semaphore_signal(barrier, inc=1, device_id=peer, device_id_type=MESH)
    pl.semaphore_wait(barrier, len(peers))


def turned(index, steps, count):
    return lax.rem(index + (steps % count), count)


def params(collective_id, vmem=None):
    return pltpu.CompilerParams(
        collective_id=collective_id, has_side_effects=True, vmem_limit_bytes=vmem
    )


def qkv_kernel(
    seq_count, exp_count, tail, q_ref, k_ref, v_ref, qr_ref, kx_ref, vx_ref,
    local_sem, z_send, z_recv, f_send, f_recv,
):
    s, e = lax.axis_index("seq"), lax.axis_index("exp")
    rows = q_ref.shape[0]
    group = qr_ref.shape[1]
    run = qr_ref.shape[0]
    arrays = ((k_ref, kx_ref, tail), (v_ref, vx_ref, tail), (q_ref, qr_ref, 0))
    enter(
        [(s, turned(e, k, exp_count)) for k in range(1, exp_count)]
        + [(turned(s, 1, seq_count), e), (turned(s, -1, seq_count), e)]
    )

    def columns(ref, index):
        return ref.at[:, pl.ds(pl.multiple_of(index * group, group), group)]

    def lines(ref, offset, index):
        return ref.at[pl.ds(pl.multiple_of(offset + index * rows, rows), rows)]

    waits = []
    for i, (source, target, offset) in enumerate(arrays):
        for k in range(1, exp_count):
            d = turned(e, k, exp_count)
            copy = remote(
                columns(source, d), lines(target, offset, e), z_send.at[i, k], z_recv.at[i, k], (s, d)
            )
            copy.start()
            waits.append(copy)
    locals_ = []
    for i, (source, target, offset) in enumerate(arrays):
        copy = pltpu.make_async_copy(columns(source, e), lines(target, offset, e), local_sem.at[i])
        copy.start()
        locals_.append(copy)

    def relay(i, k, act):
        source, target, offset = arrays[i]
        c = turned(e, -k, exp_count)
        inside = (c + 1) * rows > run - tail
        block = columns(source, e) if k == 0 else lines(target, offset, c)
        row = pl.multiple_of(lax.max(c * rows - (run - tail), 0), rows)
        copy = remote(
            block, target.at[pl.ds(row, rows)], f_send.at[i, k], f_recv.at[i, k],
            (turned(s, 1, seq_count), e),
        )
        if act == "start":
            pl.when(inside & (s < seq_count - 1))(copy.start)
        elif act == "send":
            pl.when(inside & (s < seq_count - 1))(copy.wait_send)
        else:
            pl.when(inside & (s > 0))(copy.wait_recv)

    for i in range(3):
        for k in range(exp_count):
            if k > 0:
                source, target, offset = arrays[i]
                block = lines(target, offset, turned(e, -k, exp_count))
                remote(block, block, z_send.at[i, k], z_recv.at[i, k], (s, e)).wait_recv()
            if i < 2:
                relay(i, k, "start")
    for i in range(2):
        for k in range(exp_count):
            relay(i, k, "recv")
            relay(i, k, "send")
    for copy in waits:
        copy.wait_send()
    for copy in locals_:
        copy.wait()


def exchange_qkv(queries, keys, values, seq_count, exp_count, tail):
    rows, width = queries.shape
    group, run = width // exp_count, rows * exp_count
    kind = queries.dtype
    return pl.pallas_call(
        functools.partial(qkv_kernel, seq_count, exp_count, tail),
        out_shape=(
            jax.ShapeDtypeStruct((run, group), kind),
            jax.ShapeDtypeStruct((tail + run, group), kind),
            jax.ShapeDtypeStruct((tail + run, group), kind),
        ),
        in_specs=[ANY] * 3,
        out_specs=(ANY,) * 3,
        scratch_shapes=[
            DMA((3,)),
            DMA((3, exp_count)),
            DMA((3, exp_count)),
            DMA((2, exp_count)),
            DMA((2, exp_count)),
        ],
        compiler_params=params(1),
        name="qkv_exchange",
    )(queries, keys, values)


def attend_kernel(slots, present_ref, q_ref, *refs):
    k_refs, v_refs, o_ref = refs[:slots], refs[slots : 2 * slots], refs[2 * slots]
    block = pl.program_id(0)
    scale = 1.0 / math.sqrt(q_ref.shape[1])
    q = q_ref[...]
    scores = []
    for j in range(slots):
        score = lax.dot_general(
            q, k_refs[j][...], (((1,), (1,)), ((), ())), preferred_element_type=jnp.float32
        )
        scores.append(jnp.where(present_ref[block, j] > 0, score * scale, very_negative))
    top = functools.reduce(jnp.maximum, [jnp.max(x, axis=1, keepdims=True) for x in scores])
    total, summed = 0.0, 0.0
    for j in range(slots):
        exps = jnp.exp(scores[j] - top)
        total = total + jnp.sum(exps, axis=1, keepdims=True)
        value = v_refs[j][...]
        value = jnp.where(present_ref[block, j] > 0, value, jnp.zeros_like(value))
        summed = summed + jnp.dot(
            exps.astype(jnp.bfloat16), value, preferred_element_type=jnp.float32
        )
    o_ref[...] = (summed / total).astype(o_ref.dtype)


def attend(query_run, keys_ext, values_ext, present):
    run, group = query_run.shape
    slots = present.shape[1]

    def at(slot):
        return pl.BlockSpec((BLK, HSZ), lambda block, head, flags: (block + slot, head))

    return pl.pallas_call(
        functools.partial(attend_kernel, slots),
        out_shape=jax.ShapeDtypeStruct((run, group), query_run.dtype),
        grid_spec=pltpu.PrefetchScalarGridSpec(
            num_scalar_prefetch=1,
            grid=(run // BLK, group // HSZ),
            in_specs=[at(0)] + [at(j) for j in range(slots)] * 2,
            out_specs=at(0),
        ),
        name="attend",
    )(present, query_run, *([keys_ext] * slots), *([values_ext] * slots))


def back_kernel(exp_count, a_ref, o_ref, local_sem, z_send, z_recv):
    s, e = lax.axis_index("seq"), lax.axis_index("exp")
    rows, group = o_ref.shape[0], a_ref.shape[1]
    enter([(s, turned(e, k, exp_count)) for k in range(1, exp_count)])

    def lines(index):
        return a_ref.at[pl.ds(pl.multiple_of(index * rows, rows), rows)]

    def columns(index):
        return o_ref.at[:, pl.ds(pl.multiple_of(index * group, group), group)]

    copies = []
    for k in range(1, exp_count):
        d = turned(e, k, exp_count)
        copy = remote(lines(d), columns(e), z_send.at[k], z_recv.at[k], (s, d))
        copy.start()
        copies.append(copy)
    own = pltpu.make_async_copy(lines(e), columns(e), local_sem)
    own.start()
    for k in range(1, exp_count):
        block = columns(turned(e, -k, exp_count))
        remote(block, block, z_send.at[k], z_recv.at[k], (s, e)).wait_recv()
    for copy in copies:
        copy.wait_send()
    own.wait()


def exchange_back(attended_run, exp_count):
    run, group = attended_run.shape
    return pl.pallas_call(
        functools.partial(back_kernel, exp_count),
        out_shape=jax.ShapeDtypeStruct((run // exp_count, group * exp_count), attended_run.dtype),
        in_specs=[ANY],
        out_specs=ANY,
        scratch_shapes=[DMA, DMA((exp_count,)), DMA((exp_count,))],
        compiler_params=params(2),
        name="attended_back",
    )(attended_run)


def dispatch_kernel(
    seq_count, exp_count, out_ref, rows_ref, local_sem, z_send, z_recv, x_send, x_recv, d_send, d_recv
):
    s, e = lax.axis_index("seq"), lax.axis_index("exp")
    inner_count = seq_count // OUTER
    half = out_ref.shape[2] // 2
    a, b = lax.div(s, inner_count), lax.rem(s, inner_count)
    outer = (1 - a) * inner_count + b
    forth = [a * inner_count + turned(b, j, inner_count) for j in range(1, inner_count)]
    back = [a * inner_count + turned(b, -j, inner_count) for j in range(1, inner_count)]
    across = [(1 - a) * inner_count + turned(b, -j, inner_count) for j in range(1, inner_count)]
    peers = [outer] + forth
    sources = [outer] + back
    enter(
        [(s, turned(e, k, exp_count)) for k in range(1, exp_count)] + [(p, e) for p in peers]
    )
    copies = []

    def start(copy):
        copy.start()
        copies.append(copy)

    def arrived(block, send_sem, recv_sem):
        remote(block, block, send_sem, recv_sem, (s, e)).wait_recv()

    for k in range(1, exp_count):
        d = turned(e, k, exp_count)
        start(remote(out_ref.at[d], rows_ref.at[s, e], z_send.at[k], z_recv.at[k], (s, d)))
    own = pltpu.make_async_copy(out_ref.at[e], rows_ref.at[s, e], local_sem)
    own.start()
    low, high = pl.ds(0, half), pl.ds(half, half)
    for k in range(exp_count + 1):
        if k < exp_count:
            c = turned(e, -k, exp_count)
            if k > 0:
                arrived(rows_ref.at[s, c], z_send.at[k], z_recv.at[k])
            block = out_ref.at[e] if k == 0 else rows_ref.at[s, c]
            for i, p in enumerate(peers):
                start(remote(block, rows_ref.at[s, c], x_send.at[i, k], x_recv.at[i, k], (p, e)))
        if k > 0:
            n = k - 1
            c = turned(e, -n, exp_count)
            for i, source in enumerate(sources):
                arrived(rows_ref.at[source, c], x_send.at[i, n], x_recv.at[i, n])
                if i == 0:
                    block = rows_ref.at[source, c, :, low]
                    for j, p in enumerate(forth):
                        start(remote(block, block, d_send.at[0, j, n], d_recv.at[0, j, n], (p, e)))
                else:
                    block = rows_ref.at[source, c, :, high]
                    start(
                        remote(block, block, d_send.at[1, i - 1, n], d_recv.at[1, i - 1, n], (outer, e))
                    )
    for n in range(exp_count):
        c = turned(e, -n, exp_count)
        for j, source in enumerate(across):
            for h, part in enumerate((low, high)):
                arrived(rows_ref.at[source, c, :, part], d_send.at[h, j, n], d_recv.at[h, j, n])
    for copy in copies:
        copy.wait_send()
    own.wait()


def dispatch(outgoing, seq_count, exp_count):
    inner_count = seq_count // OUTER
    return pl.pallas_call(
        functools.partial(dispatch_kernel, seq_count, exp_count),
        out_shape=jax.ShapeDtypeStruct((seq_count,) + outgoing.shape, outgoing.dtype),
        in_specs=[ANY],
        out_specs=ANY,
        scratch_shapes=[
            DMA,
            DMA((exp_count,)),
            DMA((exp_count,)),
            DMA((inner_count, exp_count)),
            DMA((inner_count, exp_count)),
            DMA((2, max(1, inner_count - 1), exp_count)),
            DMA((2, max(1, inner_count - 1), exp_count)),
        ],
        compiler_params=params(3),
        name="dispatch",
    )(outgoing)


def collect_kernel(
    seq_count, exp_count, y_ref, got_ref, own0, own1, in0, in1, out0, out1, keep0, keep1, mid0, mid1, done,
    own_sem, p_send, p_recv, m_send, m_recv, z_send, z_recv, local_sem,
):
    s, e = lax.axis_index("seq"), lax.axis_index("exp")
    inner_count = seq_count // OUTER
    half = y_ref.shape[4] // 2
    a, b = lax.div(s, inner_count), lax.rem(s, inner_count)
    other = 1 - a
    outer = other * inner_count + b
    forth = [turned(b, j, inner_count) for j in range(1, inner_count)]
    enter(
        [(s, turned(e, k, exp_count)) for k in range(1, exp_count)]
        + [(outer, e)]
        + [(a * inner_count + f, e) for f in forth]
    )
    low, high = pl.ds(0, half), pl.ds(half, half)
    copies = []

    def start(copy):
        copy.start()
        copies.append(copy)

    def arrived(block, send_sem, recv_sem):
        remote(block, block, send_sem, recv_sem, (s, e)).wait_recv()

    def chunk(k):
        return turned(e, k + 1, exp_count)

    def loads(k):
        c = chunk(k)
        return (
            pltpu.make_async_copy(y_ref.at[:, b, c, :, low], own0.at[k], own_sem.at[0, k]),
            pltpu.make_async_copy(y_ref.at[a, :, c, :, high], own1.at[k], own_sem.at[1, k]),
        )

    def first(k):
        c = chunk(k)
        start(
            remote(y_ref.at[other, :, c, :, high], in1.at[k], p_send.at[0, k], p_recv.at[0, k], (outer, e))
        )
        for j, f in enumerate(forth):
            start(
                remote(
                    y_ref.at[:, f, c, :, low], in0.at[j, k], p_send.at[1 + j, k], p_recv.at[1 + j, k],
                    (a * inner_count + f, e),
                )
            )
        for load in loads(k):
            load.start()

    def wide(ref, *index):
        return ref[index].astype(jnp.float32)

    def second(k):
        for load in loads(k):
            load.wait()
        for j in range(inner_count - 1):
            arrived(in0.at[j, k], p_send.at[1 + j, k], p_recv.at[1 + j, k])
        out0[k] = sum([wide(in0, j, k, other) for j in range(inner_count - 1)], wide(own0, k, other)).astype(
            out0.dtype
        )
        start(remote(out0.at[k], mid0.at[k], m_send.at[0, k], m_recv.at[0, k], (outer, e)))
        arrived(in1.at[k], p_send.at[0, k], p_recv.at[0, k])
        for j, f in enumerate(forth):
            out1[j, k] = (wide(own1, k, f) + wide(in1, k, f)).astype(out1.dtype)
            start(
                remote(
                    out1.at[j, k], mid1.at[j, k], m_send.at[1 + j, k], m_recv.at[1 + j, k],
                    (a * inner_count + f, e),
                )
            )
        keep0[k] = sum([wide(in0, j, k, a) for j in range(inner_count - 1)], wide(own0, k, a))
        keep1[k] = wide(own1, k, b) + wide(in1, k, b)

    def third(k):
        arrived(mid0.at[k], m_send.at[0, k], m_recv.at[0, k])
        done[k, :, low] = (keep0[k] + wide(mid0, k)).astype(done.dtype)
        for j in range(inner_count - 1):
            arrived(mid1.at[j, k], m_send.at[1 + j, k], m_recv.at[1 + j, k])
        done[k, :, high] = sum(
            [wide(mid1, j, k) for j in range(inner_count - 1)], keep1[k]
        ).astype(done.dtype)
        if k < exp_count - 1:
            start(remote(done.at[k], got_ref.at[e], z_send.at[k], z_recv.at[k], (s, chunk(k))))
        else:
            pltpu.make_async_copy(done.at[k], got_ref.at[e], local_sem).start()

    for k in range(min(AHEAD, exp_count)):
        first(k)
    for k in range(exp_count + 1):
        if k + AHEAD < exp_count:
            first(k + AHEAD)
        if k < exp_count:
            second(k)
        if k > 0:
            third(k - 1)
    for k in range(exp_count - 1):
        arrived(got_ref.at[turned(e, -k - 1, exp_count)], z_send.at[k], z_recv.at[k])
    for copy in copies:
        copy.wait_send()
    pltpu.make_async_copy(done.at[exp_count - 1], got_ref.at[e], local_sem).wait()


def collect(partials, seq_count, exp_count):
    capacity, width = partials.shape[2:]
    inner_count = seq_count // OUTER
    inner_peers = inner_count - 1
    half = width // 2
    kind = partials.dtype
    return pl.pallas_call(
        functools.partial(collect_kernel, seq_count, exp_count),
        out_shape=jax.ShapeDtypeStruct((exp_count, capacity, width), kind),
        in_specs=[ANY],
        out_specs=ANY,
        scratch_shapes=[
            pltpu.VMEM((exp_count, OUTER, capacity, half), kind),
            pltpu.VMEM((exp_count, inner_count, capacity, half), kind),
            pltpu.VMEM((inner_peers, exp_count, OUTER, capacity, half), kind),
            pltpu.VMEM((exp_count, inner_count, capacity, half), kind),
            pltpu.VMEM((exp_count, capacity, half), kind),
            pltpu.VMEM((inner_peers, exp_count, capacity, half), kind),
            pltpu.VMEM((exp_count, capacity, half), jnp.float32),
            pltpu.VMEM((exp_count, capacity, half), jnp.float32),
            pltpu.VMEM((exp_count, capacity, half), kind),
            pltpu.VMEM((inner_peers, exp_count, capacity, half), kind),
            pltpu.VMEM((exp_count, capacity, width), kind),
            DMA((2, exp_count)),
            DMA((inner_count, exp_count)),
            DMA((inner_count, exp_count)),
            DMA((inner_count, exp_count)),
            DMA((inner_count, exp_count)),
            DMA((exp_count,)),
            DMA((exp_count,)),
            DMA,
        ],
        compiler_params=params(4, 48 * 1024 * 1024),
        name="collect",
    )(partials.reshape(OUTER, inner_count, exp_count, capacity, width))


def expert_part(flat_rows, gate_slice, up_slice, down_slice):
    gate_value = jnp.dot(flat_rows, gate_slice, preferred_element_type=jnp.float32)
    up_value = jnp.dot(flat_rows, up_slice, preferred_element_type=jnp.float32)
    hidden = (jax.nn.silu(gate_value) * up_value).astype(jnp.bfloat16)
    return jnp.dot(hidden, down_slice, preferred_element_type=jnp.float32)


def per_device(
    inputs, queries, keys, values, norm_gain, expert_ids, gate_weights, pairs, w_gate, w_up, w_down
):
    rows_dev, model_width = inputs.shape
    seq_count, exp_count = lax.axis_size("seq"), lax.axis_size("exp")
    query_run, keys_ext, values_ext = exchange_qkv(
        queries, keys, values, seq_count, exp_count, DIST * BLK
    )
    blocks_dev = query_run.shape[0] // BLK
    query_block = lax.axis_index("seq") * blocks_dev + jnp.arange(blocks_dev, dtype=jnp.int32)
    key_block = query_block[:, None] - (DIST - jnp.arange(DIST + 1, dtype=jnp.int32))[None, :]
    present = jnp.any(
        (pairs[None, None, :, 0] == query_block[:, None, None])
        & (pairs[None, None, :, 1] == key_block[:, :, None]),
        axis=2,
    ).astype(jnp.int32)
    attended = exchange_back(attend(query_run, keys_ext, values_ext, present), exp_count)
    mixed_sum = inputs.astype(jnp.float32) + attended.astype(jnp.float32)
    mean_square = jnp.mean(mixed_sum * mixed_sum, axis=1, keepdims=True)
    normed = (mixed_sum * lax.rsqrt(mean_square + norm_epsilon) * norm_gain[None, :]).astype(
        jnp.bfloat16
    )
    capacity = rows_dev * TOP // exp_count
    places = exp_count * capacity
    flat_ids = expert_ids.reshape(-1)
    id_table = (flat_ids[:, None] == jnp.arange(exp_count, dtype=jnp.int32)[None, :]).astype(
        jnp.int32
    )
    ahead_count = jnp.cumsum(id_table, axis=0) - id_table
    position = jnp.sum(ahead_count * id_table, axis=1)
    target = (flat_ids * capacity + position).reshape(rows_dev, TOP)
    slots = jnp.arange(places, dtype=jnp.int32)
    spots = target[:, :, None] == slots[None, None, :]
    choose = jnp.any(spots, axis=1).astype(jnp.bfloat16)
    outgoing = (
        lax.dot_general(choose, normed, (((0,), (0,)), ((), ())), preferred_element_type=jnp.float32)
        .astype(jnp.bfloat16)
        .reshape(exp_count, capacity, model_width)
    )
    piece_rows = dispatch(outgoing, seq_count, exp_count)
    parts = expert_part(piece_rows.reshape(-1, model_width), w_gate[0], w_up[0], w_down[0])
    got = collect(parts.astype(jnp.bfloat16).reshape(piece_rows.shape), seq_count, exp_count)
    weight = jnp.sum(jnp.where(spots, gate_weights[:, :, None], 0.0), axis=1)
    coarse = weight.astype(jnp.bfloat16)
    fine = (weight - coarse.astype(jnp.float32)).astype(jnp.bfloat16)
    flat = got.reshape(places, model_width)
    combined = jnp.dot(coarse, flat, preferred_element_type=jnp.float32) + jnp.dot(
        fine, flat, preferred_element_type=jnp.float32
    )
    return (mixed_sum + combined).astype(jnp.bfloat16)


def solution(mesh):
    rows = P(("seq", "exp"), None)
    in_specs = (
        rows, rows, rows, rows, P(), rows, rows, P(),
        P("exp", None, "seq"), P("exp", None, "seq"), P("exp", "seq", None),
    )
    return jax.shard_map(
        per_device, mesh=mesh, in_specs=in_specs, out_specs=rows, check_vma=False
    )
```

time: 543 us -> 334 us (0.62); the launches traced: 532 us -> 331 us
  waiting for transfers between devices: 309 us -> 0 us
  Pallas kernels: 0 us -> 285 us
  blocking collectives: 53.4 us -> 0 us
  local copies, waits for them, and re-layouts: 35.4 us -> 1.61 us
  other arithmetic: 36.3 us -> 3.68 us
  starting transfers between devices: 31.2 us -> 0 us
  between operations: 14.3 us -> 0.21 us
  matrix products: 52.5 us -> 40.5 us
    pallas_call x0 -> x5, Pallas kernels: none -> 285 us  [the longest x1 86.1 us: collect(): pl.pallas_call(functools.partial(collect_kernel, seq_count, exp_count), o...]
    all_to_all x5 -> x0, waiting for transfers between devices: 133 us -> none  [the longest x1 48.9 us: per_device(): lax.all_to_all(slice_total.astype(jnp.bfloat16), 'exp', split_axis=0, con...]
    all_gather x1 -> x0, waiting for transfers between devices: 87.5 us -> none  [per_device(): lax.all_gather(lax.all_to_all(outgoing, 'exp', split_axis=0, concat_axis=...]
    reduce_scatter x1 -> x0, waiting for transfers between devices: 86.5 us -> none  [per_device(): lax.psum_scatter(slice_parts.astype(jnp.bfloat16), 'seq', scatter_dimensi...]
    all_to_all x1 -> x0, blocking collectives: 53.4 us -> none  [per_device(): lax.all_to_all(outgoing, 'exp', split_axis=0, concat_axis=0, tiled=True)]
    all_to_all x5 -> x0, starting transfers between devices: 23.3 us -> none  [the longest x1 6.35 us: per_device(): lax.all_to_all(values, 'exp', split_axis=1, concat_axis=0, tiled=True)]
    reduce_sum x3 -> x1, other arithmetic: 19.4 us -> 0.13 us  [per_device(): weight = jnp.sum(jnp.where(spots, gate_weights[:, :, None], 0.0), axis=1)]
    dot_general x4 -> x3, matrix products: 16.7 us -> 4.27 us  [the longest x1 2.18 us: per_device(): lax.dot_general(choose, normed, (((0,), (0,)), ((), ())), preferred_eleme...]
  transfers between devices with their start and end apart: 9 -> 0, of which waited for: 9 -> 0; matrix products, arithmetic and copies ran while one was open for 7% -> 0% of each run, Pallas kernels for 0% -> 0%
where the time goes in v1:
time: 334 us; the launch traced here: 331 us
  Pallas kernels  285 us (85%)
  matrix products  40.5 us (12%)
  other arithmetic  3.68 us (1%)
    pallas_call x1, Pallas kernels, collect(): pl.pallas_call(functools.partial(collect_kernel, seq_count, exp_count), o...  86.1 us
    pallas_call x1, Pallas kernels, dispatch(): pl.pallas_call(functools.partial(dispatch_kernel, seq_count, exp_count),...  83.9 us
    pallas_call x1, Pallas kernels, exchange_qkv(): pl.pallas_call(functools.partial(qkv_kernel, seq_count, exp_count, tail),...  69.4 us
    pallas_call x1, Pallas kernels, exchange_back(): pl.pallas_call(functools.partial(back_kernel, exp_count), out_shape=jax.S...  25.5 us
    pallas_call x1, Pallas kernels, attend(): pl.pallas_call(functools.partial(attend_kernel, slots), out_shape=jax.Sha...  20.3 us
    dot_general x1, matrix products, expert_part(): up_value = jnp.dot(flat_rows, up_slice, preferred_element_type=jnp.float32)  12.8 us
    dot_general x1, matrix products, expert_part(): jnp.dot(flat_rows, gate_slice, preferred_element_type=jnp.float32)  12.1 us
    dot_general x1, matrix products, expert_part(): return jnp.dot(hidden, down_slice, preferred_element_type=jnp.float32)  11.4 us

profile of v1, /device:TPU:0, one launch (start us, length us, event | category | flops | bytes accessed | tf_op | source)
XLA Modules:
  0.0 331.2 jit_solution(15050710738856983435)
XLA Ops:
  0.0 0.8 slice_bitcast_fusion.1
  0.8 0.1 broadcast_compare_fusion
  0.8 0.1 broadcast_subtract_fusion
  0.9 0.2 and_reduce_fusion
  1.1 0.6 convert_element_type.42.present_ref
  1.7 69.4 %qkv_exchange.1 = (bf16[1024,512]{1,0:T(8,128)(2,1)}, bf16[2048,512]{1,0:T(8,128)(2,1)}, bf16[2048,512]{1,0:T(8,128)(2,1)}) custom-call(bf16[128,4096]{1,0:T(8,128)(2,1)} %q_ref.1, bf16[128,4096]{1,0:T(8,128)(2,1)} %k_ref.1, bf16[128,4096]{1,0:T(8,128)(2,1)} %v_ref.1), custom_call_target="tpu_custom_call" | custom-call | tf_op jit(solution)/shard_map/qkv_exchange/pallas_call | solution.py:128
  71.1 20.3 %attend.1.a_ref = bf16[1024,512]{1,0:T(8,128)(2,1)} custom-call(s32[2,3]{1,0:T(2,128)} %convert_element_type.42.present_ref, bf16[1024,512]{1,0:T(8,128)(2,1)} %get-tuple-element.8.q_ref, bf16[2048,512]{1,0:T(8,128)(2,1)} %get-tuple-element.9.refs_0_.refs_1_.refs_2_, bf16[2048,512]{1,0:T(8,128)(2,1)} %get-tuple-element.9.refs_0_.refs_1_.refs_2_, ...), custom_call_target="tpu_custom_call" | custom-call | tf_op jit(solution)/shard_map/attend/pallas_call | solution.py:180
  91.4 0.0 copy-start.1
  91.4 0.0 copy-start.4
  91.4 0.0 copy-start.3
  91.4 25.5 %attended_back.1 = bf16[128,4096]{1,0:T(8,128)(2,1)} custom-call(bf16[1024,512]{1,0:T(8,128)(2,1)} %attend.1.a_ref), custom_call_target="tpu_custom_call" | custom-call | tf_op jit(solution)/shard_map/attended_back/pallas_call | solution.py:222
  116.9 0.0 copy-done.1
  116.9 0.0 copy-start
  116.9 1.7 multiply_reduce_fusion
  118.7 0.0 copy-done.4
  118.7 0.1 copy.24
  118.8 0.1 eq.85
  119.0 0.6 reduce-window.6
  119.6 0.2 slice_reduce_fusion
  119.8 0.1 eq.81
  120.0 0.1 fusion.20
  120.0 0.1 reduce_sum.30
  120.2 0.1 copy.26
  120.3 0.1 fusion.15
  120.4 0.0 copy-done.3
  120.4 0.0 copy-done
  120.4 2.2 convolution_convert_fusion
  122.6 83.9 %dispatch.1 = bf16[4,8,32,4096]{3,2,1,0:T(8,128)(2,1)} custom-call(bf16[8,32,4096]{2,1,0:T(8,128)(2,1)} %bitcast.40), custom_call_target="tpu_custom_call" | custom-call | tf_op jit(solution)/shard_map/dispatch/pallas_call | solution.py:298
  206.5 0.0 copy-start.2
  206.5 0.0 slice-start
  206.5 12.8 %fusion.2 = f32[1024,1024]{1,0:T(8,128)S(1)} fusion(bf16[1024,4096]{1,0:T(8,128)(2,1)} %bitcast.37, bf16[1,4096,1024]{2,1,0:T(8,128)(2,1)} %param.20), kind=kOutput, calls=%fused_computation.2 | convolution fusion | flops 8589934592 | bytes 20971520 | tf_op jit(solution)/shard_map/dot_general | solution.py:460
  219.3 0.0 copy-done.2
  219.3 0.0 slice-start.1
  219.3 12.1 %multiply_convert_fusion = bf16[1024,1024]{1,0:T(8,128)(2,1)S(1)} fusion(f32[1024,1024]{1,0:T(8,128)S(1)} %fusion.2, bf16[1024,4096]{1,0:T(8,128)(2,1)S(1)} %bitcast.38, bf16[1,4096,1024]{2,1,0:T(8,128)(2,1)} %param.19), kind=kOutput, calls=%fused_computation.11 | convolution fusion | flops 8596226048 | bytes 23068672 | tf_op jit(solution)/shard_map/dot_general | solution.py:459
  231.4 0.0 slice-done
  231.4 0.0 slice-done.1
  231.4 11.4 %fusion.6 = bf16[1024,4096]{1,0:T(8,128)(2,1)} fusion(bf16[1024,1024]{1,0:T(8,128)(2,1)S(1)} %multiply_convert_fusion, bf16[1,1024,4096]{2,1,0:T(8,128)(2,1)S(1)} %bitcast.42), kind=kOutput, calls=%fused_computation.6 | convolution fusion | flops 8594128896 | bytes 18874368 | tf_op jit(solution)/shard_map/dot_general | solution.py:462
  242.8 0.0 copy-start.5
  242.8 86.1 %collect.1 = bf16[8,32,4096]{2,1,0:T(8,128)(2,1)S(1)} custom-call(bf16[2,2,8,32,4096]{4,3,2,1,0:T(8,128)(2,1)} %bitcast.39), custom_call_target="tpu_custom_call" | custom-call | tf_op jit(solution)/shard_map/collect/pallas_call | solution.py:427
  328.9 0.0 copy-done.5
  328.9 0.1 select_reduce_fusion
  329.1 0.4 fusion.17
  329.5 1.6 fusion.10
  (8 shorter events, 0.1 us)
Async XLA Ops:
  91.4 25.6 %copy-start.1 = (bf16[128,4096]{1,0:T(8,128)(2,1)S(1)}, bf16[128,4096]{1,0:T(8,128)(2,1)}, u32[]{:S(2)}) copy-start(bf16[128,4096]{1,0:T(8,128)(2,1)} %param.11) | copy-start | bytes 3145732
  91.4 27.3 %copy-start.4 = (s32[128,2]{0,1:T(2,128)S(1)}, s32[128,2]{0,1:T(2,128)}, u32[]{:S(2)}) copy-start(s32[128,2]{0,1:T(2,128)} %param.16) | copy-start | bytes 3076
  91.4 29.0 %copy-start.3 = (f32[4096]{0:T(1024)S(1)}, f32[4096]{0:T(1024)}, u32[]{:S(2)}) copy-start(f32[4096]{0:T(1024)} %param.15) | copy-start | bytes 49156
  116.9 3.5 %copy-start = (bf16[128,4096]{1,0:T(8,128)(2,1)S(1)}, bf16[128,4096]{1,0:T(8,128)(2,1)}, u32[]{:S(2)}) copy-start(bf16[128,4096]{1,0:T(8,128)(2,1)} %attended_back.1) | copy-start | bytes 3145732
  206.5 12.8 %copy-start.2 = (bf16[4,8,32,4096]{3,2,1,0:T(8,128)(2,1)S(1)}, bf16[4,8,32,4096]{3,2,1,0:T(8,128)(2,1)}, u32[]{:S(2)}) copy-start(bf16[4,8,32,4096]{3,2,1,0:T(8,128)(2,1)} %dispatch.1) | copy-start | bytes 25165828
  206.5 24.9 %slice-start = ((s8[8388608]{0:T(1024)(128)(4,1)}), s8[4194304]{0:T(1024)(128)(4,1)S(1)}, s32[]{:S(2)}) async-start(s8[8388608]{0:T(1024)(128)(4,1)} %bitcast.41), calls=%async_computation | async-start | bytes 8388608
  219.3 12.1 %slice-start.1 = ((s8[8388608]{0:T(1024)(128)(4,1)}), s8[4194304]{0:T(1024)(128)(4,1)S(1)}, s32[]{:S(2)}) async-start(s8[8388608]{0:T(1024)(128)(4,1)} %bitcast.41), calls=%async_computation.1 | async-start | bytes 8388608
  242.8 86.1 %copy-start.5 = (f32[128,2]{0,1:T(2,128)S(1)}, f32[128,2]{0,1:T(2,128)}, u32[]{:S(2)}) copy-start(f32[128,2]{0,1:T(2,128)} %param.17) | copy-start | bytes 3076

commit v2 on v1

--- a/solution.py
+++ b/solution.py
@@ -13,7 +13,6 @@
 BLK = 512
 DIST = 2
 OUTER = 2
-AHEAD = 2
 
 very_negative = -1e30
 norm_epsilon = 1e-05
@@ -230,236 +229,271 @@
     )(attended_run)
 
 
-def dispatch_kernel(
-    seq_count, exp_count, out_ref, rows_ref, local_sem, z_send, z_recv, x_send, x_recv, d_send, d_recv
+def experts_kernel(
+    seq_count, exp_count, together, tile, wide_tile,
+    out_ref, gate_hbm, up_hbm, down_hbm, got_ref,
+    gate_ref, up_ref, down_ref, buf, x_ref, hid_ref, in0, in1, out0, out1, mid0, mid1, done,
+    local_sem, w_sem, z_send, z_recv, x_send, x_recv, d_send, d_recv,
+    p_send, p_recv, m_send, m_recv, g_send, g_recv,
 ):
     s, e = lax.axis_index("seq"), lax.axis_index("exp")
     inner_count = seq_count // OUTER
-    half = out_ref.shape[2] // 2
+    capacity, width = out_ref.shape[1:]
+    half = width // 2
     a, b = lax.div(s, inner_count), lax.rem(s, inner_count)
-    outer = (1 - a) * inner_count + b
-    forth = [a * inner_count + turned(b, j, inner_count) for j in range(1, inner_count)]
-    back = [a * inner_count + turned(b, -j, inner_count) for j in range(1, inner_count)]
-    across = [(1 - a) * inner_count + turned(b, -j, inner_count) for j in range(1, inner_count)]
-    peers = [outer] + forth
-    sources = [outer] + back
-    enter(
-        [(s, turned(e, k, exp_count)) for k in range(1, exp_count)] + [(p, e) for p in peers]
-    )
-    copies = []
-
-    def start(copy):
-        copy.start()
-        copies.append(copy)
+    other = 1 - a
+    outer = (other * inner_count + b, e)
+    steps = range(1, inner_count)
+    forth = [turned(b, j, inner_count) for j in steps]
+    back = [turned(b, -j, inner_count) for j in steps]
+    inner = [(a * inner_count + f, e) for f in forth]
+    low, high = pl.ds(0, half), pl.ds(half, half)
+    groups = exp_count // together
+    chunk_rows = seq_count * capacity
+
+    def chunk(k):
+        return lax.rem(e - k + exp_count, exp_count)
 
     def arrived(block, send_sem, recv_sem):
         remote(block, block, send_sem, recv_sem, (s, e)).wait_recv()
 
-    for k in range(1, exp_count):
-        d = turned(e, k, exp_count)
-        start(remote(out_ref.at[d], rows_ref.at[s, e], z_send.at[k], z_recv.at[k], (s, d)))
-    own = pltpu.make_async_copy(out_ref.at[e], rows_ref.at[s, e], local_sem)
+    weights = [
+        pltpu.make_async_copy(source.at[0], target, w_sem.at[i])
+        for i, (source, target) in enumerate(
+            ((gate_hbm, gate_ref), (up_hbm, up_ref), (down_hbm, down_ref))
+        )
+    ]
+    own = pltpu.make_async_copy(out_ref.at[e], buf.at[a, b, e], local_sem)
     own.start()
-    low, high = pl.ds(0, half), pl.ds(half, half)
-    for k in range(exp_count + 1):
-        if k < exp_count:
-            c = turned(e, -k, exp_count)
-            if k > 0:
-                arrived(rows_ref.at[s, c], z_send.at[k], z_recv.at[k])
-            block = out_ref.at[e] if k == 0 else rows_ref.at[s, c]
-            for i, p in enumerate(peers):
-                start(remote(block, rows_ref.at[s, c], x_send.at[i, k], x_recv.at[i, k], (p, e)))
-        if k > 0:
+    enter([(s, turned(e, k, exp_count)) for k in range(1, exp_count)] + [outer] + inner)
+
+    def spread(k):
+        d = lax.rem(e + k, exp_count)
+        return remote(out_ref.at[d], buf.at[a, b, e], z_send.at[k], z_recv.at[k], (s, d))
+
+    def directs(k):
+        block = buf.at[a, b, chunk(k)]
+        return [
+            remote(block, block, x_send.at[i, k], x_recv.at[i, k], peer)
+            for i, peer in enumerate([outer] + inner)
+        ]
+
+    def relays(k):
+        c = chunk(k)
+        copies = []
+        for j, peer in enumerate(inner):
+            block = buf.at[other, b, c, :, low]
+            copies.append(remote(block, block, d_send.at[0, j, k], d_recv.at[0, j, k], peer))
+            block = buf.at[a, back[j], c, :, high]
+            copies.append(remote(block, block, d_send.at[1, j, k], d_recv.at[1, j, k], outer))
+        return copies
+
+    def gather_step(k):
+        @pl.when(k < exp_count)
+        def _():
+            @pl.when(k > 0)
+            def _():
+                arrived(buf.at[a, b, chunk(k)], z_send.at[k], z_recv.at[k])
+
+            for copy in directs(k):
+                copy.start()
+
+        @pl.when((k > 0) & (k <= exp_count))
+        def _():
             n = k - 1
-            c = turned(e, -n, exp_count)
-            for i, source in enumerate(sources):
-                arrived(rows_ref.at[source, c], x_send.at[i, n], x_recv.at[i, n])
-                if i == 0:
-                    block = rows_ref.at[source, c, :, low]
-                    for j, p in enumerate(forth):
-                        start(remote(block, block, d_send.at[0, j, n], d_recv.at[0, j, n], (p, e)))
-                else:
-                    block = rows_ref.at[source, c, :, high]
-                    start(
-                        remote(block, block, d_send.at[1, i - 1, n], d_recv.at[1, i - 1, n], (outer, e))
-                    )
-    for n in range(exp_count):
-        c = turned(e, -n, exp_count)
-        for j, source in enumerate(across):
+            c = chunk(n)
+            arrived(buf.at[other, b, c], x_send.at[0, n], x_recv.at[0, n])
+            for j in range(inner_count - 1):
+                arrived(buf.at[a, back[j], c], x_send.at[1 + j, n], x_recv.at[1 + j, n])
+            for copy in relays(n):
+                copy.start()
+
+    def complete(k):
+        c = chunk(k)
+        for j in range(inner_count - 1):
             for h, part in enumerate((low, high)):
-                arrived(rows_ref.at[source, c, :, part], d_send.at[h, j, n], d_recv.at[h, j, n])
-    for copy in copies:
-        copy.wait_send()
-    own.wait()
-
-
-def dispatch(outgoing, seq_count, exp_count):
-    inner_count = seq_count // OUTER
-    return pl.pallas_call(
-        functools.partial(dispatch_kernel, seq_count, exp_count),
-        out_shape=jax.ShapeDtypeStruct((seq_count,) + outgoing.shape, outgoing.dtype),
-        in_specs=[ANY],
-        out_specs=ANY,
-        scratch_shapes=[
-            DMA,
-            DMA((exp_count,)),
-            DMA((exp_count,)),
-            DMA((inner_count, exp_count)),
-            DMA((inner_count, exp_count)),
-            DMA((2, max(1, inner_count - 1), exp_count)),
-            DMA((2, max(1, inner_count - 1), exp_count)),
-        ],
-        compiler_params=params(3),
-        name="dispatch",
-    )(outgoing)
-
-
-def collect_kernel(
-    seq_count, exp_count, y_ref, got_ref, own0, own1, in0, in1, out0, out1, keep0, keep1, mid0, mid1, done,
-    own_sem, p_send, p_recv, m_send, m_recv, z_send, z_recv, local_sem,
-):
-    s, e = lax.axis_index("seq"), lax.axis_index("exp")
-    inner_count = seq_count // OUTER
-    half = y_ref.shape[4] // 2
-    a, b = lax.div(s, inner_count), lax.rem(s, inner_count)
-    other = 1 - a
-    outer = other * inner_count + b
-    forth = [turned(b, j, inner_count) for j in range(1, inner_count)]
-    enter(
-        [(s, turned(e, k, exp_count)) for k in range(1, exp_count)]
-        + [(outer, e)]
-        + [(a * inner_count + f, e) for f in forth]
-    )
-    low, high = pl.ds(0, half), pl.ds(half, half)
-    copies = []
-
-    def start(copy):
-        copy.start()
-        copies.append(copy)
-
-    def arrived(block, send_sem, recv_sem):
-        remote(block, block, send_sem, recv_sem, (s, e)).wait_recv()
-
-    def chunk(k):
-        return turned(e, k + 1, exp_count)
-
-    def loads(k):
-        c = chunk(k)
-        return (
-            pltpu.make_async_copy(y_ref.at[:, b, c, :, low], own0.at[k], own_sem.at[0, k]),
-            pltpu.make_async_copy(y_ref.at[a, :, c, :, high], own1.at[k], own_sem.at[1, k]),
-        )
+                arrived(buf.at[other, back[j], c, :, part], d_send.at[h, j, k], d_recv.at[h, j, k])
 
     def first(k):
         c = chunk(k)
-        start(
-            remote(y_ref.at[other, :, c, :, high], in1.at[k], p_send.at[0, k], p_recv.at[0, k], (outer, e))
-        )
-        for j, f in enumerate(forth):
-            start(
-                remote(
-                    y_ref.at[:, f, c, :, low], in0.at[j, k], p_send.at[1 + j, k], p_recv.at[1 + j, k],
-                    (a * inner_count + f, e),
+        return [
+            remote(buf.at[other, :, c, :, high], in1.at[k], p_send.at[0, k], p_recv.at[0, k], outer)
+        ] + [
+            remote(
+                buf.at[:, f, c, :, low], in0.at[j, k], p_send.at[1 + j, k], p_recv.at[1 + j, k], inner[j]
+            )
+            for j, f in enumerate(forth)
+        ]
+
+    def second(k):
+        return [remote(out0.at[k], mid0.at[k], m_send.at[0, k], m_recv.at[0, k], outer)] + [
+            remote(out1.at[j, k], mid1.at[j, k], m_send.at[1 + j, k], m_recv.at[1 + j, k], inner[j])
+            for j in range(inner_count - 1)
+        ]
+
+    def third(k):
+        return remote(done.at[k], got_ref.at[e], g_send.at[k], g_recv.at[k], (s, chunk(k)))
+
+    def stay():
+        return pltpu.make_async_copy(done.at[0], got_ref.at[e], local_sem)
+
+    def wide(value):
+        return value.astype(jnp.float32)
+
+    def inner_sum(k, side):
+        total = wide(buf[side, b, chunk(k), :, low])
+        for j in range(inner_count - 1):
+            total = total + wide(in0[j, k, side])
+        return total
+
+    def outer_sum(k, lane):
+        return wide(buf[a, lane, chunk(k), :, high]) + wide(in1[k, lane])
+
+    def sum_step(k):
+        @pl.when((k >= 0) & (k < exp_count))
+        def _():
+            sends = second(k)
+            for j in range(inner_count - 1):
+                arrived(in0.at[j, k], p_send.at[1 + j, k], p_recv.at[1 + j, k])
+            out0[k] = inner_sum(k, other).astype(out0.dtype)
+            sends[0].start()
+            arrived(in1.at[k], p_send.at[0, k], p_recv.at[0, k])
+            for j, f in enumerate(forth):
+                out1[j, k] = outer_sum(k, f).astype(out1.dtype)
+                sends[1 + j].start()
+
+        @pl.when((k > 0) & (k <= exp_count))
+        def _():
+            n = k - 1
+            arrived(mid0.at[n], m_send.at[0, n], m_recv.at[0, n])
+            done[n, :, low] = (inner_sum(n, a) + wide(mid0[n])).astype(done.dtype)
+            total = outer_sum(n, b)
+            for j in range(inner_count - 1):
+                arrived(mid1.at[j, n], m_send.at[1 + j, n], m_recv.at[1 + j, n])
+                total = total + wide(mid1[j, n])
+            done[n, :, high] = total.astype(done.dtype)
+
+            @pl.when(n == 0)
+            def _():
+                stay().start()
+
+            @pl.when(n > 0)
+            def _():
+                third(n).start()
+
+    def loop(begin, end, body):
+        def step(i, carry):
+            body(i)
+            return carry
+
+        lax.fori_loop(begin, end, step, 0)
+
+    loop(1, exp_count, lambda k: spread(k).start())
+    own.wait()
+    for copy in weights:
+        copy.start()
+    loop(0, together + 2, gather_step)
+    for copy in weights:
+        copy.wait()
+    tiles, wide_tiles = hid_ref.shape[1] // tile, width // wide_tile
+    stride, wide_stride = max(1, tiles // together), max(1, wide_tiles // together)
+
+    def group(p):
+        base = p * together
+        for i in range(together):
+            complete(base + i)
+            x_ref[pl.ds(i * chunk_rows, chunk_rows)] = buf[:, :, chunk(base + i)].reshape(chunk_rows, width)
+
+        def hidden_tile(n):
+            where = pl.ds(pl.multiple_of(n * tile, tile), tile)
+            x = x_ref[...]
+            gate = jnp.dot(x, gate_ref[:, where], preferred_element_type=jnp.float32)
+            up = jnp.dot(x, up_ref[:, where], preferred_element_type=jnp.float32)
+            hid_ref[:, where] = (jax.nn.silu(gate) * up).astype(hid_ref.dtype)
+
+            @pl.when(lax.rem(n, stride) == 0)
+            def _():
+                gather_step(base + together + 2 + lax.div(n, stride))
+
+        loop(0, tiles, hidden_tile)
+        for i in range(together):
+            for copy in directs(base + i) + relays(base + i):
+                copy.wait_send()
+
+        def down_tile(n):
+            where = pl.ds(pl.multiple_of(n * wide_tile, wide_tile), wide_tile)
+            y = jnp.dot(hid_ref[...], down_ref[:, where], preferred_element_type=jnp.float32).astype(buf.dtype)
+            for i in range(together):
+                buf[:, :, chunk(base + i), :, where] = y[i * chunk_rows : (i + 1) * chunk_rows].reshape(
+                    OUTER, inner_count, capacity, wide_tile
                 )
-            )
-        for load in loads(k):
-            load.start()
-
-    def wide(ref, *index):
-        return ref[index].astype(jnp.float32)
-
-    def second(k):
-        for load in loads(k):
-            load.wait()
-        for j in range(inner_count - 1):
-            arrived(in0.at[j, k], p_send.at[1 + j, k], p_recv.at[1 + j, k])
-        out0[k] = sum([wide(in0, j, k, other) for j in range(inner_count - 1)], wide(own0, k, other)).astype(
-            out0.dtype
-        )
-        start(remote(out0.at[k], mid0.at[k], m_send.at[0, k], m_recv.at[0, k], (outer, e)))
-        arrived(in1.at[k], p_send.at[0, k], p_recv.at[0, k])
-        for j, f in enumerate(forth):
-            out1[j, k] = (wide(own1, k, f) + wide(in1, k, f)).astype(out1.dtype)
-            start(
-                remote(
-                    out1.at[j, k], mid1.at[j, k], m_send.at[1 + j, k], m_recv.at[1 + j, k],
-                    (a * inner_count + f, e),
-                )
-            )
-        keep0[k] = sum([wide(in0, j, k, a) for j in range(inner_count - 1)], wide(own0, k, a))
-        keep1[k] = wide(own1, k, b) + wide(in1, k, b)
-
-    def third(k):
-        arrived(mid0.at[k], m_send.at[0, k], m_recv.at[0, k])
-        done[k, :, low] = (keep0[k] + wide(mid0, k)).astype(done.dtype)
-        for j in range(inner_count - 1):
-            arrived(mid1.at[j, k], m_send.at[1 + j, k], m_recv.at[1 + j, k])
-        done[k, :, high] = sum(
-            [wide(mid1, j, k) for j in range(inner_count - 1)], keep1[k]
-        ).astype(done.dtype)
-        if k < exp_count - 1:
-            start(remote(done.at[k], got_ref.at[e], z_send.at[k], z_recv.at[k], (s, chunk(k))))
-        else:
-            pltpu.make_async_copy(done.at[k], got_ref.at[e], local_sem).start()
-
-    for k in range(min(AHEAD, exp_count)):
-        first(k)
-    for k in range(exp_count + 1):
-        if k + AHEAD < exp_count:
-            first(k + AHEAD)
-        if k < exp_count:
-            second(k)
-        if k > 0:
-            third(k - 1)
-    for k in range(exp_count - 1):
-        arrived(got_ref.at[turned(e, -k - 1, exp_count)], z_send.at[k], z_recv.at[k])
-    for copy in copies:
-        copy.wait_send()
-    pltpu.make_async_copy(done.at[exp_count - 1], got_ref.at[e], local_sem).wait()
-
-
-def collect(partials, seq_count, exp_count):
-    capacity, width = partials.shape[2:]
+
+            @pl.when(lax.rem(n, wide_stride) == 0)
+            def _():
+                sum_step(base - 2 * together + lax.div(n, wide_stride))
+
+        loop(0, wide_tiles, down_tile)
+        for i in range(together):
+            for copy in first(base + i):
+                copy.start()
+
+    loop(0, groups, group)
+    loop(max(0, groups - 2) * together, exp_count + 1, sum_step)
+
+    def finish(k):
+        for copy in first(k) + second(k):
+            copy.wait_send()
+
+        @pl.when(k > 0)
+        def _():
+            spread(k).wait_send()
+            third(k).wait_send()
+            arrived(got_ref.at[lax.rem(e + k, exp_count)], g_send.at[k], g_recv.at[k])
+
+    loop(0, exp_count, finish)
+    stay().wait()
+
+
+def experts(outgoing, w_gate, w_up, w_down, seq_count, exp_count):
+    exp_count, capacity, width = outgoing.shape
+    hidden = w_gate.shape[2]
     inner_count = seq_count // OUTER
     inner_peers = inner_count - 1
     half = width // 2
-    kind = partials.dtype
+    kind = outgoing.dtype
+    together = 1
+    while 2 * together * seq_count * capacity <= 256 and exp_count % (2 * together) == 0:
+        together *= 2
+    rows = together * seq_count * capacity
+    tile, wide_tile = min(256, hidden // together), min(512, width // together)
+    vmem = [
+        w_gate.shape[1:],
+        w_up.shape[1:],
+        w_down.shape[1:],
+        (OUTER, inner_count, exp_count, capacity, width),
+        (rows, width),
+        (rows, hidden),
+        (inner_peers, exp_count, OUTER, capacity, half),
+        (exp_count, inner_count, capacity, half),
+        (exp_count, capacity, half),
+        (inner_peers, exp_count, capacity, half),
+        (exp_count, capacity, half),
+        (inner_peers, exp_count, capacity, half),
+        (exp_count, capacity, width),
+    ]
+    one, per_peer, per_side = (exp_count,), (inner_count, exp_count), (2, inner_peers, exp_count)
+    sems = [one, one, per_peer, per_peer, per_side, per_side, per_peer, per_peer, per_peer, per_peer, one, one]
     return pl.pallas_call(
-        functools.partial(collect_kernel, seq_count, exp_count),
+        functools.partial(experts_kernel, seq_count, exp_count, together, tile, wide_tile),
         out_shape=jax.ShapeDtypeStruct((exp_count, capacity, width), kind),
-        in_specs=[ANY],
+        in_specs=[ANY] * 4,
         out_specs=ANY,
-        scratch_shapes=[
-            pltpu.VMEM((exp_count, OUTER, capacity, half), kind),
-            pltpu.VMEM((exp_count, inner_count, capacity, half), kind),
-            pltpu.VMEM((inner_peers, exp_count, OUTER, capacity, half), kind),
-            pltpu.VMEM((exp_count, inner_count, capacity, half), kind),
-            pltpu.VMEM((exp_count, capacity, half), kind),
-            pltpu.VMEM((inner_peers, exp_count, capacity, half), kind),
-            pltpu.VMEM((exp_count, capacity, half), jnp.float32),
-            pltpu.VMEM((exp_count, capacity, half), jnp.float32),
-            pltpu.VMEM((exp_count, capacity, half), kind),
-            pltpu.VMEM((inner_peers, exp_count, capacity, half), kind),
-            pltpu.VMEM((exp_count, capacity, width), kind),
-            DMA((2, exp_count)),
-            DMA((inner_count, exp_count)),
-            DMA((inner_count, exp_count)),
-            DMA((inner_count, exp_count)),
-            DMA((inner_count, exp_count)),
-            DMA((exp_count,)),
-            DMA((exp_count,)),
-            DMA,
-        ],
-        compiler_params=params(4, 48 * 1024 * 1024),
-        name="collect",
-    )(partials.reshape(OUTER, inner_count, exp_count, capacity, width))
-
-
-def expert_part(flat_rows, gate_slice, up_slice, down_slice):
-    gate_value = jnp.dot(flat_rows, gate_slice, preferred_element_type=jnp.float32)
-    up_value = jnp.dot(flat_rows, up_slice, preferred_element_type=jnp.float32)
-    hidden = (jax.nn.silu(gate_value) * up_value).astype(jnp.bfloat16)
-    return jnp.dot(hidden, down_slice, preferred_element_type=jnp.float32)
+        scratch_shapes=[pltpu.VMEM(shape, kind) for shape in vmem]
+        + [DMA, DMA((3,))]
+        + [DMA(shape) for shape in sems],
+        compiler_params=params(3, 60 * 1024 * 1024),
+        name="experts",
+    )(outgoing, w_gate, w_up, w_down)
 
 
 def per_device(
@@ -501,9 +535,7 @@
         .astype(jnp.bfloat16)
         .reshape(exp_count, capacity, model_width)
     )
-    piece_rows = dispatch(outgoing, seq_count, exp_count)
-    parts = expert_part(piece_rows.reshape(-1, model_width), w_gate[0], w_up[0], w_down[0])
-    got = collect(parts.astype(jnp.bfloat16).reshape(piece_rows.shape), seq_count, exp_count)
+    got = experts(outgoing, w_gate, w_up, w_down, seq_count, exp_count)
     weight = jnp.sum(jnp.where(spots, gate_weights[:, :, None], 0.0), axis=1)
     coarse = weight.astype(jnp.bfloat16)
     fine = (weight - coarse.astype(jnp.float32)).astype(jnp.bfloat16)

time: 334 us -> 306 us (0.916)
  matrix products: 40.5 us -> 6.08 us
  Pallas kernels: 285 us -> 294 us
    dot_general x3 -> x0, matrix products: 36.2 us -> none  [the longest x1 12.8 us: expert_part(): up_value = jnp.dot(flat_rows, up_slice, preferred_element_type=jnp.float32)]
    pallas_call x2 -> x1, Pallas kernels: 170 us -> 179 us  [experts(): pl.pallas_call(functools.partial(experts_kernel, seq_count, exp_count, to...]
where the time goes in v2:
time: 306 us
  Pallas kernels  294 us (96%)
  matrix products  6.08 us (2%)
  other arithmetic  3.68 us (1%)
    pallas_call x1, Pallas kernels, experts(): pl.pallas_call(functools.partial(experts_kernel, seq_count, exp_count, to...  179 us
    pallas_call x1, Pallas kernels, exchange_qkv(): pl.pallas_call(functools.partial(qkv_kernel, seq_count, exp_count, tail),...  69.4 us
    pallas_call x1, Pallas kernels, exchange_back(): pl.pallas_call(functools.partial(back_kernel, exp_count), out_shape=jax.S...  25.5 us
    pallas_call x1, Pallas kernels, attend(): pl.pallas_call(functools.partial(attend_kernel, slots), out_shape=jax.Sha...  20.3 us

profile of v2, /device:TPU:0, one launch (start us, length us, event | category | flops | bytes accessed | tf_op | source)
XLA Modules:
  0.0 305.7 jit_solution(7091919438694282837)
XLA Ops:
  0.0 0.8 slice_bitcast_fusion.1
  0.8 0.1 broadcast_compare_fusion
  0.8 0.1 broadcast_subtract_fusion
  0.9 0.2 and_reduce_fusion
  1.1 0.6 convert_element_type.36.present_ref
  1.7 69.4 %qkv_exchange.1 = (bf16[1024,512]{1,0:T(8,128)(2,1)}, bf16[2048,512]{1,0:T(8,128)(2,1)}, bf16[2048,512]{1,0:T(8,128)(2,1)}) custom-call(bf16[128,4096]{1,0:T(8,128)(2,1)} %q_ref.1, bf16[128,4096]{1,0:T(8,128)(2,1)} %k_ref.1, bf16[128,4096]{1,0:T(8,128)(2,1)} %v_ref.1), custom_call_target="tpu_custom_call" | custom-call | tf_op jit(solution)/shard_map/qkv_exchange/pallas_call | solution.py:127
  71.1 20.3 %attend.1.a_ref = bf16[1024,512]{1,0:T(8,128)(2,1)} custom-call(s32[2,3]{1,0:T(2,128)} %convert_element_type.36.present_ref, bf16[1024,512]{1,0:T(8,128)(2,1)} %get-tuple-element.8.q_ref, bf16[2048,512]{1,0:T(8,128)(2,1)} %get-tuple-element.9.refs_0_.refs_1_.refs_2_, bf16[2048,512]{1,0:T(8,128)(2,1)} %get-tuple-element.9.refs_0_.refs_1_.refs_2_, ...), custom_call_target="tpu_custom_call" | custom-call | tf_op jit(solution)/shard_map/attend/pallas_call | solution.py:179
  91.4 0.0 copy-start.2
  91.4 0.0 copy-start.4
  91.4 0.0 copy-start.3
  91.4 25.5 %attended_back.1 = bf16[128,4096]{1,0:T(8,128)(2,1)} custom-call(bf16[1024,512]{1,0:T(8,128)(2,1)} %attend.1.a_ref), custom_call_target="tpu_custom_call" | custom-call | tf_op jit(solution)/shard_map/attended_back/pallas_call | solution.py:221
  116.9 0.0 copy-done.2
  116.9 0.0 copy-start.1
  116.9 1.7 multiply_reduce_fusion
  118.7 0.0 copy-done.4
  118.7 0.1 copy.24
  118.8 0.1 eq.85
  119.0 0.6 reduce-window.6
  119.6 0.2 slice_reduce_fusion
  119.8 0.1 eq.81
  120.0 0.1 fusion.9
  120.0 0.1 reduce_sum.30
  120.2 0.1 copy.26
  120.3 0.1 fusion.4
  120.4 0.0 copy-done.3
  120.4 0.0 copy-done.1
  120.4 2.1 convolution_convert_fusion
  122.6 0.0 copy-start.5
  122.6 179.1 %experts.1 = bf16[8,32,4096]{2,1,0:T(8,128)(2,1)} custom-call(bf16[8,32,4096]{2,1,0:T(8,128)(2,1)} %bitcast.19, bf16[1,4096,1024]{2,1,0:T(8,128)(2,1)} %gate_hbm.1, bf16[1,4096,1024]{2,1,0:T(8,128)(2,1)} %up_hbm.1, bf16[1,1024,4096]{2,1,0:T(8,128)(2,1)} %down_hbm.1), custom_call_target="tpu_custom_call" | custom-call | tf_op jit(solution)/shard_map/experts/pallas_call | solution.py:486
  301.6 0.0 copy-done.5
  301.6 0.1 select_reduce_fusion
  301.8 0.0 copy-start
  301.8 2.2 fusion.6
  304.0 0.0 copy-done
  304.0 1.8 fusion.1
  (7 shorter events, 0.1 us)
Async XLA Ops:
  91.4 25.6 %copy-start.2 = (bf16[128,4096]{1,0:T(8,128)(2,1)S(1)}, bf16[128,4096]{1,0:T(8,128)(2,1)}, u32[]{:S(2)}) copy-start(bf16[128,4096]{1,0:T(8,128)(2,1)} %param.11) | copy-start | bytes 3145732
  91.4 27.3 %copy-start.4 = (s32[128,2]{0,1:T(2,128)S(1)}, s32[128,2]{0,1:T(2,128)}, u32[]{:S(2)}) copy-start(s32[128,2]{0,1:T(2,128)} %param.16) | copy-start | bytes 3076
  91.4 29.0 %copy-start.3 = (f32[4096]{0:T(1024)S(1)}, f32[4096]{0:T(1024)}, u32[]{:S(2)}) copy-start(f32[4096]{0:T(1024)} %param.15) | copy-start | bytes 49156
  116.9 3.5 %copy-start.1 = (bf16[128,4096]{1,0:T(8,128)(2,1)S(1)}, bf16[128,4096]{1,0:T(8,128)(2,1)}, u32[]{:S(2)}) copy-start(bf16[128,4096]{1,0:T(8,128)(2,1)} %attended_back.1) | copy-start | bytes 3145732
  122.6 179.1 %copy-start.5 = (f32[128,2]{0,1:T(2,128)S(1)}, f32[128,2]{0,1:T(2,128)}, u32[]{:S(2)}) copy-start(f32[128,2]{0,1:T(2,128)} %param.17) | copy-start | bytes 3076
  301.8 2.2 copy-start

commit v3 on v2

--- a/solution.py
+++ b/solution.py
@@ -145,88 +145,99 @@
     )(queries, keys, values)
 
 
-def attend_kernel(slots, present_ref, q_ref, *refs):
-    k_refs, v_refs, o_ref = refs[:slots], refs[slots : 2 * slots], refs[2 * slots]
-    block = pl.program_id(0)
-    scale = 1.0 / math.sqrt(q_ref.shape[1])
-    q = q_ref[...]
-    scores = []
-    for j in range(slots):
-        score = lax.dot_general(
-            q, k_refs[j][...], (((1,), (1,)), ((), ())), preferred_element_type=jnp.float32
+def attend_kernel(
+    seq_count, exp_count, slots, present_ref, q_ref, k_ref, v_ref, o_ref, att_ref, local_sem, z_send, z_recv
+):
+    s, e = lax.axis_index("seq"), lax.axis_index("exp")
+    rows = o_ref.shape[0]
+    run, group = q_ref.shape
+    heads, blocks, owners = group // HSZ, run // BLK, BLK // rows
+    scale = 1.0 / math.sqrt(HSZ)
+    enter([(s, turned(e, k, exp_count)) for k in range(1, exp_count)])
+
+    def source(owner, head):
+        return att_ref.at[
+            pl.ds(pl.multiple_of(owner * rows, rows), rows), pl.ds(pl.multiple_of(head * HSZ, HSZ), HSZ)
+        ]
+
+    def target(giver, head):
+        return o_ref.at[:, pl.ds(pl.multiple_of(giver * group + head * HSZ, HSZ), HSZ)]
+
+    def send(owner, head):
+        return remote(
+            source(owner, head), target(e, head), z_send.at[owner, head], z_recv.at[e, head], (s, owner)
         )
-        scores.append(jnp.where(present_ref[block, j] > 0, score * scale, very_negative))
-    top = functools.reduce(jnp.maximum, [jnp.max(x, axis=1, keepdims=True) for x in scores])
-    total, summed = 0.0, 0.0
-    for j in range(slots):
-        exps = jnp.exp(scores[j] - top)
-        total = total + jnp.sum(exps, axis=1, keepdims=True)
-        value = v_refs[j][...]
-        value = jnp.where(present_ref[block, j] > 0, value, jnp.zeros_like(value))
-        summed = summed + jnp.dot(
-            exps.astype(jnp.bfloat16), value, preferred_element_type=jnp.float32
-        )
-    o_ref[...] = (summed / total).astype(o_ref.dtype)
-
-
-def attend(query_run, keys_ext, values_ext, present):
+
+    def own(head):
+        return pltpu.make_async_copy(source(e, head), target(e, head), local_sem.at[head])
+
+    def step(i, carry):
+        head = lax.rem(i, heads)
+        block = lax.rem(lax.div(e, owners) + 1 + lax.div(i, heads), blocks)
+        column = pl.ds(pl.multiple_of(head * HSZ, HSZ), HSZ)
+
+        def lines(slot):
+            return pl.ds(pl.multiple_of((block + slot) * BLK, BLK), BLK)
+
+        q = q_ref[lines(0), column]
+        scores = []
+        for j in range(slots):
+            score = lax.dot_general(
+                q, k_ref[lines(j), column], (((1,), (1,)), ((), ())), preferred_element_type=jnp.float32
+            )
+            scores.append(jnp.where(present_ref[block, j] > 0, score * scale, very_negative))
+        top = functools.reduce(jnp.maximum, [jnp.max(x, axis=1, keepdims=True) for x in scores])
+        total, summed = 0.0, 0.0
+        for j in range(slots):
+            exps = jnp.exp(scores[j] - top)
+            total = total + jnp.sum(exps, axis=1, keepdims=True)
+            value = v_ref[lines(j), column]
+            value = jnp.where(present_ref[block, j] > 0, value, jnp.zeros_like(value))
+            summed = summed + jnp.dot(
+                exps.astype(jnp.bfloat16), value, preferred_element_type=jnp.float32
+            )
+        att_ref[lines(0), column] = (summed / total).astype(att_ref.dtype)
+        for j in range(owners):
+            owner = block * owners + j
+
+            @pl.when(owner != e)
+            def _():
+                send(owner, head).start()
+
+            @pl.when(owner == e)
+            def _():
+                own(head).start()
+
+        return carry
+
+    lax.fori_loop(0, blocks * heads, step, 0)
+    for head in range(heads):
+        for k in range(1, exp_count):
+            giver, owner = turned(e, -k, exp_count), turned(e, k, exp_count)
+            block = target(giver, head)
+            remote(block, block, z_send.at[giver, head], z_recv.at[giver, head], (s, e)).wait_recv()
+            send(owner, head).wait_send()
+        own(head).wait()
+
+
+def attend(query_run, keys_ext, values_ext, present, seq_count, exp_count):
     run, group = query_run.shape
-    slots = present.shape[1]
-
-    def at(slot):
-        return pl.BlockSpec((BLK, HSZ), lambda block, head, flags: (block + slot, head))
-
+    heads = group // HSZ
+    held = pl.BlockSpec(memory_space=pltpu.VMEM)
     return pl.pallas_call(
-        functools.partial(attend_kernel, slots),
-        out_shape=jax.ShapeDtypeStruct((run, group), query_run.dtype),
-        grid_spec=pltpu.PrefetchScalarGridSpec(
-            num_scalar_prefetch=1,
-            grid=(run // BLK, group // HSZ),
-            in_specs=[at(0)] + [at(j) for j in range(slots)] * 2,
-            out_specs=at(0),
-        ),
+        functools.partial(attend_kernel, seq_count, exp_count, present.shape[1]),
+        out_shape=jax.ShapeDtypeStruct((run // exp_count, group * exp_count), query_run.dtype),
+        in_specs=[pl.BlockSpec(memory_space=pltpu.SMEM)] + [held] * 3,
+        out_specs=ANY,
+        scratch_shapes=[
+            pltpu.VMEM((run, group), query_run.dtype),
+            DMA((heads,)),
+            DMA((exp_count, heads)),
+            DMA((exp_count, heads)),
+        ],
+        compiler_params=params(2, 48 * 1024 * 1024),
         name="attend",
-    )(present, query_run, *([keys_ext] * slots), *([values_ext] * slots))
-
-
-def back_kernel(exp_count, a_ref, o_ref, local_sem, z_send, z_recv):
-    s, e = lax.axis_index("seq"), lax.axis_index("exp")
-    rows, group = o_ref.shape[0], a_ref.shape[1]
-    enter([(s, turned(e, k, exp_count)) for k in range(1, exp_count)])
-
-    def lines(index):
-        return a_ref.at[pl.ds(pl.multiple_of(index * rows, rows), rows)]
-
-    def columns(index):
-        return o_ref.at[:, pl.ds(pl.multiple_of(index * group, group), group)]
-
-    copies = []
-    for k in range(1, exp_count):
-        d = turned(e, k, exp_count)
-        copy = remote(lines(d), columns(e), z_send.at[k], z_recv.at[k], (s, d))
-        copy.start()
-        copies.append(copy)
-    own = pltpu.make_async_copy(lines(e), columns(e), local_sem)
-    own.start()
-    for k in range(1, exp_count):
-        block = columns(turned(e, -k, exp_count))
-        remote(block, block, z_send.at[k], z_recv.at[k], (s, e)).wait_recv()
-    for copy in copies:
-        copy.wait_send()
-    own.wait()
-
-
-def exchange_back(attended_run, exp_count):
-    run, group = attended_run.shape
-    return pl.pallas_call(
-        functools.partial(back_kernel, exp_count),
-        out_shape=jax.ShapeDtypeStruct((run // exp_count, group * exp_count), attended_run.dtype),
-        in_specs=[ANY],
-        out_specs=ANY,
-        scratch_shapes=[DMA, DMA((exp_count,)), DMA((exp_count,))],
-        compiler_params=params(2),
-        name="attended_back",
-    )(attended_run)
+    )(present, query_run, keys_ext, values_ext)
 
 
 def experts_kernel(
@@ -430,7 +441,7 @@
 
             @pl.when(lax.rem(n, wide_stride) == 0)
             def _():
-                sum_step(base - 2 * together + lax.div(n, wide_stride))
+                sum_step(base - together + lax.div(n, wide_stride))
 
         loop(0, wide_tiles, down_tile)
         for i in range(together):
@@ -438,7 +449,7 @@
                 copy.start()
 
     loop(0, groups, group)
-    loop(max(0, groups - 2) * together, exp_count + 1, sum_step)
+    loop((groups - 1) * together, exp_count + 1, sum_step)
 
     def finish(k):
         for copy in first(k) + second(k):
@@ -512,7 +523,7 @@
         & (pairs[None, None, :, 1] == key_block[:, :, None]),
         axis=2,
     ).astype(jnp.int32)
-    attended = exchange_back(attend(query_run, keys_ext, values_ext, present), exp_count)
+    attended = attend(query_run, keys_ext, values_ext, present, seq_count, exp_count)
     mixed_sum = inputs.astype(jnp.float32) + attended.astype(jnp.float32)
     mean_square = jnp.mean(mixed_sum * mixed_sum, axis=1, keepdims=True)
     normed = (mixed_sum * lax.rsqrt(mean_square + norm_epsilon) * norm_gain[None, :]).astype(

time: 306 us -> 286 us (0.935)
  Pallas kernels: 294 us -> 273 us
    pallas_call x2 -> x1, Pallas kernels: 45.8 us -> 34.5 us  [attend(): pl.pallas_call(functools.partial(attend_kernel, seq_count, exp_count, pre...]
    pallas_call x1, Pallas kernels: 179 us -> 169 us  [experts(): pl.pallas_call(functools.partial(experts_kernel, seq_count, exp_count, to...]
where the time goes in v3:
time: 286 us
  Pallas kernels  273 us (95%)
  matrix products  6.15 us (2%)
  local copies, waits for them, and re-layouts  4.63 us (2%)
    pallas_call x1, Pallas kernels, experts(): pl.pallas_call(functools.partial(experts_kernel, seq_count, exp_count, to...  169 us
    pallas_call x1, Pallas kernels, exchange_qkv(): pl.pallas_call(functools.partial(qkv_kernel, seq_count, exp_count, tail),...  69.5 us
    pallas_call x1, Pallas kernels, attend(): pl.pallas_call(functools.partial(attend_kernel, seq_count, exp_count, pre...  34.5 us

profile of v3, /device:TPU:0, one launch (start us, length us, event | category | flops | bytes accessed | tf_op | source)
XLA Modules:
  0.0 285.8 jit_solution(15362279719797539780)
XLA Ops:
  0.0 0.8 slice_bitcast_fusion.1
  0.8 0.1 broadcast_compare_fusion
  0.8 0.1 broadcast_subtract_fusion
  0.9 0.2 and_reduce_fusion
  1.1 69.5 %qkv_exchange.1 = (bf16[1024,512]{1,0:T(8,128)(2,1)}, bf16[2048,512]{1,0:T(8,128)(2,1)}, bf16[2048,512]{1,0:T(8,128)(2,1)}) custom-call(bf16[128,4096]{1,0:T(8,128)(2,1)} %q_ref.1, bf16[128,4096]{1,0:T(8,128)(2,1)} %k_ref.1, bf16[128,4096]{1,0:T(8,128)(2,1)} %v_ref.1), custom_call_target="tpu_custom_call" | custom-call | tf_op jit(solution)/shard_map/qkv_exchange/pallas_call | solution.py:127
  70.6 0.0 copy-start
  70.6 1.6 copy-done
  72.2 0.0 copy-start.1
  72.2 1.2 copy-done.1
  73.4 0.0 copy-start.3
  73.4 34.5 %attend.1 = bf16[128,4096]{1,0:T(8,128)(2,1)S(1)} custom-call(s32[2,3]{1,0:T(2,128)S(1)} %convert_element_type.36.present_ref, bf16[1024,512]{1,0:T(8,128)(2,1)S(1)} %copy-done.1, bf16[2048,512]{1,0:T(8,128)(2,1)S(1)} %copy-done, bf16[2048,512]{1,0:T(8,128)(2,1)} %get-tuple-element.10.v_ref), custom_call_target="tpu_custom_call" | custom-call | tf_op jit(solution)/shard_map/attend/pallas_call | solution.py:227
  107.9 0.0 copy-done.3
  107.9 0.0 copy-start.5
  107.9 0.0 copy-start.4
  107.9 0.4 multiply_reduce_fusion
  108.4 0.2 copy-done.5
  108.6 0.1 copy.24
  108.7 0.1 eq.85
  108.9 0.6 reduce-window.6
  109.4 0.2 slice_reduce_fusion
  109.7 0.1 eq.81
  109.8 0.1 fusion.9
  109.9 0.1 reduce_sum.30
  110.1 0.1 copy.26
  110.2 0.1 fusion.4
  110.3 0.0 copy-done.4
  110.3 2.2 convolution_convert_fusion
  112.5 0.0 copy-start.6
  112.5 169.2 %experts.1 = bf16[8,32,4096]{2,1,0:T(8,128)(2,1)} custom-call(bf16[8,32,4096]{2,1,0:T(8,128)(2,1)} %bitcast.19, bf16[1,4096,1024]{2,1,0:T(8,128)(2,1)} %gate_hbm.1, bf16[1,4096,1024]{2,1,0:T(8,128)(2,1)} %up_hbm.1, bf16[1,1024,4096]{2,1,0:T(8,128)(2,1)} %down_hbm.1), custom_call_target="tpu_custom_call" | custom-call | tf_op jit(solution)/shard_map/experts/pallas_call | solution.py:497
  281.7 0.0 copy-done.6
  281.7 0.1 select_reduce_fusion
  281.8 0.0 copy-start.2
  281.8 2.2 fusion.6
  284.0 0.0 copy-done.2
  284.1 1.8 fusion.1
  (8 shorter events, 0.1 us)
Async XLA Ops:
  70.6 1.6 copy-start
  72.2 1.2 copy-start.1
  73.4 34.5 %copy-start.3 = (bf16[128,4096]{1,0:T(8,128)(2,1)S(1)}, bf16[128,4096]{1,0:T(8,128)(2,1)}, u32[]{:S(2)}) copy-start(bf16[128,4096]{1,0:T(8,128)(2,1)} %param.11) | copy-start | bytes 3145732
  107.9 0.7 copy-start.5
  107.9 2.4 copy-start.4
  112.5 169.2 %copy-start.6 = (f32[128,2]{0,1:T(2,128)S(1)}, f32[128,2]{0,1:T(2,128)}, u32[]{:S(2)}) copy-start(f32[128,2]{0,1:T(2,128)} %param.17) | copy-start | bytes 3076
  281.8 2.2 copy-start.2
